TPU v7x, 768 devices: a whole 4x8x12 slice. The times are simulated.
768 devices in a mesh: blk: 48 (over z, y_lo), patch: 16 (over x, y_hi, core).
Axes of the slice: x: 4, y: 8 (y_hi: 2, y_lo: 4; y = y_hi * 4 + y_lo), z: 12, core: 2. Of those that a mesh axis runs over, the one named last changes fastest.
Arguments:
- queries: bfloat16 [24576, 8192], P('blk', 'patch'), may hold values from -6 to 6
- keys: bfloat16 [6144, 1024], P('blk'), may hold values from -6 to 6
- values: bfloat16 [6144, 1024], P('blk'), may hold values from -6 to 6
- outputs: bfloat16 [24576, 8192], P('blk', 'patch'), may hold values from -6 to 6
- out_grad: bfloat16 [24576, 8192], P('blk', 'patch'), may hold values from -6 to 6
- lse: float32 [24576, 64], P('blk', 'patch'), may hold values from 5 to 7
- doc_ids: int32 [24576], P('blk'), may hold values from 0 to 5, never falling along the last dimension, each value on 1 to 12288 neighbouring positions
- image_docs: int32 [48], replicated, may hold values from 0 to 5
Outputs:
- query_grad: bfloat16 [24576, 8192], P('blk', 'patch')
- kv_grad: bfloat16 [6144, 2048], P(('blk', 'patch'))
Inputs may be any that keep to these rules, and one draw needn't show every extreme that they name: `doc_ids`: documents are runs of consecutive tokens, numbered in order; one document holds exactly 12288 tokens. `image_docs`: the image rows of block b are rows b * 128 to (b + 1) * 128 - 1.
All inputs are finite; a program needn't handle non-finite values.
Results may differ from a plain program's by a relative error of at most 0.0049.
Values may be sent and summed in bfloat16 or wider, within the bound.
No kernel may reach another device: no remote copies, remote signals or barrier semaphores. Data moves between devices by JAX's collectives and lax.ppermute only.
A program may use at most 64 MiB of HBM per device.

v0:
```python
import jax
import jax.numpy as jnp
from jax import lax
from jax.sharding import Mesh
from jax.sharding import PartitionSpec as P

BLK = ("blk_0", "blk_1")
BLK_PATCH = ("blk_0", "blk_1", "patch")


def in_one_piece(arrays, axis, dim, along):
    both = jnp.concatenate(arrays, axis=along)
    filled, at, outs = (lax.all_gather(both, axis, axis=dim, tiled=True), 0, [])
    for a in arrays:
        outs.append(lax.slice_in_dim(filled, at, at + a.shape[along], axis=along))
        at += a.shape[along]
    return tuple(outs)


def summed_rows(array, axes, dim):
    for axis in axes:
        array = lax.psum_scatter(array, axis, scatter_dimension=dim, tiled=True)
    return array


def body(queries, keys, values, outputs, out_grad, lse, doc_ids, image_docs):
    cycle_size = lax.axis_size(BLK)
    patch_size = lax.axis_size("patch")
    head_col = lax.axis_index("patch")
    tok_rows = queries.shape[0]
    local_heads = lse.shape[1]
    head_size = queries.shape[1] // local_heads
    all_heads = local_heads * patch_size
    kv_heads = keys.shape[1] // head_size
    group = all_heads // kv_heads
    sub_group = min(local_heads, group)
    kv_local = local_heads // sub_group
    sharers = group // sub_group
    kv_width = kv_local * head_size
    image_rows = keys.shape[0]
    scaling = head_size ** (-0.5)
    first_kv = head_col * local_heads // group
    key_local = lax.dynamic_slice_in_dim(keys, first_kv * head_size, kv_width, 1)
    value_local = lax.dynamic_slice_in_dim(values, first_kv * head_size, kv_width, 1)
    query_four = queries.reshape(tok_rows, kv_local, sub_group, head_size)
    grad_four = out_grad.reshape(tok_rows, kv_local, sub_group, head_size)
    output_four = outputs.reshape(tok_rows, kv_local, sub_group, head_size)
    delta = jnp.sum(grad_four.astype(jnp.float32) * output_four.astype(jnp.float32), axis=3)
    delta_t = jnp.transpose(delta, (1, 2, 0))[..., None]
    stats = jnp.transpose(lse.reshape(tok_rows, kv_local, sub_group), (1, 2, 0))[..., None]

    def tile(key_blk, value_blk, dkey, dvalue, dquery, block_doc):
        active = doc_ids == block_doc

        def work(carried):
            dkey_in, dvalue_in, dquery_in = carried
            key_three = key_blk.reshape(-1, kv_local, head_size)
            value_three = value_blk.reshape(-1, kv_local, head_size)
            score = (
                jnp.einsum(
                    "tgsd,igd->gsti", query_four, key_three, preferred_element_type=jnp.float32
                )
                * scaling
            )
            prob_full = jnp.where(active[:, None], jnp.exp(score - stats), 0.0)
            dprob = jnp.einsum(
                "tgsd,igd->gsti", grad_four, value_three, preferred_element_type=jnp.float32
            )
            dscore = (prob_full * (dprob - delta_t) * scaling).astype(jnp.bfloat16)
            prob_low = prob_full.astype(jnp.bfloat16)
            dquery_out = dquery_in + jnp.einsum(
                "gsti,igd->tgsd", dscore, key_three, preferred_element_type=jnp.float32
            )
            dkey_out = jnp.einsum(
                "gsti,tgsd->igd", dscore, query_four, preferred_element_type=jnp.float32
            )
            dvalue_out = jnp.einsum(
                "gsti,tgsd->igd", prob_low, grad_four, preferred_element_type=jnp.float32
            )
            return (dkey_out, dvalue_out, dquery_out)

        def skip(carried):
            return carried

        return lax.cond(jnp.any(active), work, skip, (dkey, dvalue, dquery))

    dquery_zero = jnp.zeros((tok_rows, kv_local, sub_group, head_size), jnp.float32)
    key_every, value_every = in_one_piece((key_local, value_local), BLK, 0, 1)
    full_zero = jnp.zeros((image_rows * cycle_size, kv_local, head_size), jnp.float32)
    block_zero = jnp.zeros((image_rows, kv_local, head_size), jnp.float32)

    def local_step(blk_pos, carry):
        dkey_all, dvalue_all, dquery = carry
        row_start = blk_pos * image_rows
        key_blk = lax.dynamic_slice_in_dim(key_every, row_start, image_rows, 0)
        value_blk = lax.dynamic_slice_in_dim(value_every, row_start, image_rows, 0)
        dkey_blk, dvalue_blk, dquery = tile(
            key_blk, value_blk, block_zero, block_zero, dquery, image_docs[blk_pos]
        )
        dkey_all = lax.dynamic_update_slice_in_dim(dkey_all, dkey_blk, row_start, 0)
        dvalue_all = lax.dynamic_update_slice_in_dim(dvalue_all, dvalue_blk, row_start, 0)
        return (dkey_all, dvalue_all, dquery)

    dkey_all, dvalue_all, dquery = lax.fori_loop(
        0, cycle_size, local_step, (full_zero, full_zero, dquery_zero)
    )
    dkey_home, dvalue_home = (summed_rows(dkey_all, BLK, 0), summed_rows(dvalue_all, BLK, 0))
    query_grad = dquery.reshape(tok_rows, local_heads * head_size).astype(jnp.bfloat16)
    partial_value = jnp.stack([dkey_home, dvalue_home], axis=2).reshape(
        image_rows, kv_local * 2 * head_size
    )
    received = lax.all_to_all(partial_value, "patch", split_axis=0, concat_axis=1, tiled=True)
    owner_rows = received.shape[0]
    summed = jnp.sum(received.reshape(owner_rows, kv_heads, sharers, 2 * head_size), axis=2)
    kv_grad = summed.reshape(owner_rows, kv_heads * 2 * head_size).astype(jnp.bfloat16)
    return (query_grad, kv_grad)


def solution(mesh):
    torus = Mesh(mesh.devices.reshape(12, 4, mesh.shape["patch"]), ("blk_0", "blk_1", "patch"))
    placed = (
        P(BLK, "patch"),
        P(BLK, None),
        P(BLK, None),
        P(BLK, "patch"),
        P(BLK, "patch"),
        P(BLK, "patch"),
        P(BLK),
        P(),
    )
    return jax.shard_map(
        body,
        mesh=torus,
        in_specs=placed,
        out_specs=(P(BLK, "patch"), P(BLK_PATCH, None)),
        check_vma=False,
    )
```

profile of v0, /device:TPU:1, one launch (start us, length us, event | category | flops | bytes accessed | tf_op | source)
XLA Modules:
  0.0 705.1 jit_solution(10172261802225630762)
XLA Ops:
  12.2 202.8 %all-gather.2.cloned.1.call-done = bf16[6144,256]{1,0:T(8,128)(2,1)} async-done(((bf16[128,256]{1,0:T(8,128)(2,1)}), bf16[6144,256]{1,0:T(8,128)(2,1)}) %all-gather.2.cloned.1.call-update) | async-done | bytes 3145744 | tf_op jit(solution)/shard_map/all_gather | solution.py:13
  215.1 3.8 fusion.27
  219.0 1.9 broadcast_in_dim.32.clone
  220.9 1.8 broadcast_in_dim.32
  222.7 210.3 %while.20 = (s32[]{:T(128)}, f32[6144,1,128]{2,0,1:T(8,128)}, f32[6144,1,128]{2,0,1:T(8,128)}, f32[512,1,4,128]{0,3,2,1:T(8,128)S(1)}, s32[48]{0:T(128)S(1)}, /*...) while((s32[]{:T(128)}, f32[6144,1,128]{2,0,1:T(8,128)}, ...), condition=%wide.region_5.6_spmd, body=%wide.region_1.5_spmd.sunk | while | flops 337904640 | bytes 9426241 | solution.py:104
  223.3 1.3 fusion.31
  228.6 3.9 conditional.2
  233.7 1.3 fusion.31
  235.7 3.9 conditional.2
  242.8 3.9 conditional.2
  247.9 1.3 fusion.31
  256.4 3.9 conditional.2
  271.3 1.3 fusion.31
  289.6 3.9 conditional.2
  294.7 1.3 fusion.31
  296.7 3.9 conditional.2
  301.8 1.3 fusion.31
  305.1 1.3 fusion.31
  308.3 1.3 fusion.31
  310.3 3.9 conditional.2
  315.4 1.3 fusion.31
  322.0 1.3 fusion.31
  327.2 3.9 conditional.2
  338.9 1.3 fusion.31
  340.8 3.9 conditional.2
  346.0 1.3 fusion.31
  349.2 1.3 fusion.31
  352.5 1.3 fusion.31
  355.8 1.3 fusion.31
  357.7 3.9 conditional.2
  366.1 1.3 fusion.31
  374.6 3.9 conditional.2
  381.7 3.9 conditional.2
  390.1 1.3 fusion.31
  393.4 1.3 fusion.31
  399.9 1.3 fusion.31
  405.1 3.9 conditional.2
  410.3 1.3 fusion.31
  413.5 1.3 fusion.31
  423.3 1.3 fusion.31
  425.3 3.9 conditional.2
  430.4 1.3 fusion.31
  433.9 107.3 %reduce-scatter.5.cloned.1.call-done = f32[512,1,128]{2,0,1:T(8,128)} async-done(((f32[6144,1,128]{2,0,1:T(8,128)}), f32[512,1,128]{2,0,1:T(8,128)}) %reduce-scatter.5.cloned.1.call-update) | async-done | bytes 262160 | tf_op jit(solution)/shard_map/reduce_scatter | solution.py:22
  541.3 67.2 %reduce-scatter.9.cloned.1.call-done = f32[512,1,128]{2,0,1:T(8,128)} async-done(((f32[6144,1,128]{2,0,1:T(8,128)}), f32[512,1,128]{2,0,1:T(8,128)}) %reduce-scatter.9.cloned.1.call-update) | async-done | bytes 262160 | tf_op jit(solution)/shard_map/reduce_scatter | solution.py:22
  608.5 36.1 %reduce-scatter.7.cloned.1.call-done = f32[128,1,128]{2,0,1:T(8,128)} async-done(((f32[512,1,128]{2,0,1:T(8,128)}), f32[128,1,128]{2,0,1:T(8,128)}) %reduce-scatter.7.cloned.1.call-update) | async-done | bytes 65552 | tf_op jit(solution)/shard_map/reduce_scatter | solution.py:22
  644.6 32.2 %reduce-scatter.11.cloned.1.call-done = f32[128,1,128]{2,0,1:T(8,128)} async-done(((f32[512,1,128]{2,0,1:T(8,128)}), f32[128,1,128]{2,0,1:T(8,128)}) %reduce-scatter.11.cloned.1.call-update) | async-done | bytes 65552 | tf_op jit(solution)/shard_map/reduce_scatter | solution.py:22
  678.6 9.3 %all-to-all-start = ((f32[16,8,256]{2,1,0:T(8,128)}), f32[16,8,256]{2,1,0:T(8,128)S(1)}, u32[]{:S(2)}, u32[]{:S(2)}) async-start(f32[16,8,256]{2,1,0:T(8,128)} %all_to_all.12), calls=%async_computation.4 | async-start | bytes 262144 | tf_op jit(solution)/shard_map/all_to_all | solution.py:112
  689.0 8.9 %all-to-all-done = f32[16,8,256]{2,1,0:T(8,128)S(1)} async-done(((f32[16,8,256]{2,1,0:T(8,128)}), f32[16,8,256]{2,1,0:T(8,128)S(1)}, u32[]{:S(2)}, u32[]{:S(2)}) %all-to-all-start) | async-done | bytes 131104 | tf_op jit(solution)/shard_map/all_to_all | solution.py:112
  (326 shorter events, 158.1 us)
Async XLA Ops:
  7.2 4.4 copy-start
  7.2 207.9 %all-gather.2.cloned.1.call-start = ((), (), s32[]{:S(2)}) async-start(), calls=%async_computation.5 | async-start | bytes 3211264 | tf_op jit(solution)/shard_map/all_gather | solution.py:13
  8.7 532.5 %reduce-scatter.5.cloned.1.call-start = ((), (), s32[]{:S(2)}) async-start(), calls=%async_computation.6 | async-start | bytes 3407872 | tf_op jit(solution)/shard_map/reduce_scatter | solution.py:22
  219.0 3.8 copy-start.1
  219.0 3.8 copy-start.2
  219.0 3.8 copy-start.3
  433.1 175.4 %reduce-scatter.9.cloned.1.call-start = ((), (), s32[]{:S(2)}) async-start(), calls=%async_computation.8 | async-start | bytes 3407872 | tf_op jit(solution)/shard_map/reduce_scatter | solution.py:22
  433.8 210.8 %reduce-scatter.7.cloned.1.call-start = ((), (), s32[]{:S(2)}) async-start(), calls=%async_computation.7 | async-start | bytes 327680 | tf_op jit(solution)/shard_map/reduce_scatter | solution.py:22
  541.2 135.6 %reduce-scatter.11.cloned.1.call-start = ((), (), s32[]{:S(2)}) async-start(), calls=%async_computation.9 | async-start | bytes 327680 | tf_op jit(solution)/shard_map/reduce_scatter | solution.py:22
  678.6 19.3 %all-to-all-start = ((f32[16,8,256]{2,1,0:T(8,128)}), f32[16,8,256]{2,1,0:T(8,128)S(1)}, u32[]{:S(2)}, u32[]{:S(2)}) async-start(f32[16,8,256]{2,1,0:T(8,128)} %all_to_all.12), calls=%async_computation.4 | async-start | bytes 262144 | tf_op jit(solution)/shard_map/all_to_all | solution.py:112
Sparse Core Ops, SparseCore 0:
  10.9 204.0 all-gather.1
  433.2 107.9 reduce-scatter.4
  544.3 64.1 reduce-scatter.8
  611.4 33.1 reduce-scatter.6
  647.5 29.2 reduce-scatter.10
where the time goes:
time: 710 us; the launch traced here: 705 us
  waiting for transfers between devices  455 us (64%)
  local copies, waits for them, and re-layouts  73.7 us (10%)
  other arithmetic  66.1 us (9%)
  matrix products  53.8 us (8%)
  loops' own time  32.7 us (5%)
  between operations  13.9 us (2%)
  starting transfers between devices  9.51 us (1%)
    reduce_scatter x4, waiting for transfers between devices, summed_rows(): array = lax.psum_scatter(array, axis, scatter_dimension=dim, tiled=True)  243 us
    all_gather x1, waiting for transfers between devices, in_one_piece(): filled, at, outs = (lax.all_gather(both, axis, axis=dim, tiled=True), 0, [])  203 us
    reduce_or x48, other arithmetic, tile(): return lax.cond(jnp.any(active), work, skip, (dkey, dvalue, dquery))  63.7 us
    dynamic_update_slice x48, local copies, waits for them, and re-layouts, local_step(): lax.dynamic_update_slice_in_dim(dvalue_all, dvalue_blk, row_start, 0)  31.8 us
    another operation x1, loops' own time, body(): lax.fori_loop(0, cycle_size, local_step, (full_zero, full_zero, dquery_ze...  30.8 us
    dynamic_slice x48, local copies, waits for them, and re-layouts, local_step(): image_docs[blk_pos]  27.9 us
    dot_general x14, matrix products, work(): jnp.einsum('tgsd,igd->gsti', query_four, key_three, preferred_element_typ...  15.6 us
    dot_general x14, matrix products, work(): jnp.einsum('gsti,igd->tgsd', dscore, key_three, preferred_element_type=jn...  15.3 us
  transfers between devices with their start and end apart: 6, of which 6 were waited for; matrix products, arithmetic and copies ran while one was open for 1% of the time, Pallas kernels for 0%

commit v1 on v0

v1 whole, which is shorter than its diff:
```python
import functools
import math

import jax
import jax.numpy as jnp
from jax import lax
from jax.experimental import pallas as pl
from jax.experimental.pallas import tpu as pltpu
from jax.sharding import Mesh
from jax.sharding import PartitionSpec as P

BLK = ("z", "yl")
PATCH = ("x", "yh", "c")
DOC_SLOTS = 8
PAD_DOC = 7
GROUP = 4
MASKED = 1e30


def dot_nt(a, b):
    return lax.dot_general(a, b, (((1,), (1,)), ((), ())), preferred_element_type=jnp.float32)


def dot_nn(a, b):
    return lax.dot_general(a, b, (((1,), (0,)), ((), ())), preferred_element_type=jnp.float32)


def grad_kernel(span, block_docs, q_own, q_oth, g_own, g_oth, stat_own, stat_oth, docs, keys, values,
                dq_own, dq_oth, dkv, lse_doc, dq_acc, k_grp, v_grp, kt_grp, dk_acc, dv_acc, active, active_doc,
                *, heads, head_size):
    blocks, half_rows, _ = keys.shape
    scaling = head_size ** (-0.5)
    log2e = math.log2(math.e)

    doc_row = docs[...]
    for d in range(DOC_SLOTS):
        inside = doc_row == d
        for s, stat in enumerate((stat_own, stat_oth)):
            lse_doc[d, s * heads:(s + 1) * heads, :] = jnp.where(inside, stat[heads:, :] * log2e, MASKED)
    dq_acc[...] = jnp.zeros_like(dq_acc)
    dkv[...] = jnp.zeros_like(dkv)

    lowest, highest = span[0], span[1]

    def collect(b, count):
        doc = block_docs[b]
        active[count] = b
        active_doc[count] = doc
        return count + jnp.where((doc >= lowest) & (doc <= highest), 1, 0)

    count = lax.fori_loop(0, blocks, collect, jnp.int32(0))
    for s in range(GROUP):
        active[count + s] = 0
        active_doc[count + s] = PAD_DOC

    def group_step(grp, carry):
        base = grp * GROUP
        for s in range(GROUP):
            b = active[base + s]
            k_grp[s * half_rows:(s + 1) * half_rows, :] = keys[b]
            v_grp[s * half_rows:(s + 1) * half_rows, :] = values[b]
        kt_grp[...] = k_grp[...].T
        dk_acc[...] = jnp.zeros_like(dk_acc)
        dv_acc[...] = jnp.zeros_like(dv_acc)
        for h in range(2 * heads):
            q_ref, g_ref, stat = (q_own, g_own, stat_own) if h < heads else (q_oth, g_oth, stat_oth)
            col = (h % heads) * head_size
            query = q_ref[:, col:col + head_size]
            grad = g_ref[:, col:col + head_size]
            delta = stat[h % heads:h % heads + 1, :]
            score = dot_nt(k_grp[...], query)
            dprob = dot_nt(v_grp[...], grad)
            probs, dscores = [], []
            for s in range(GROUP):
                rows = slice(s * half_rows, (s + 1) * half_rows)
                stats = lse_doc[active_doc[base + s], h:h + 1, :]
                prob = jnp.exp2(score[rows] * (scaling * log2e) - stats)
                probs.append(prob.astype(jnp.bfloat16))
                dscores.append((prob * (dprob[rows] - delta) * scaling).astype(jnp.bfloat16))
            prob_low = jnp.concatenate(probs, axis=0)
            dscore = jnp.concatenate(dscores, axis=0)
            dk_acc[...] += dot_nn(dscore, query)
            dv_acc[...] += dot_nn(prob_low, grad)
            dq_acc[h] += dot_nn(kt_grp[...], dscore)
        for s in range(GROUP):
            rows = slice(s * half_rows, (s + 1) * half_rows)

            @pl.when(base + s < count)
            def _():
                b = active[base + s]
                dkv[b, :, :head_size] = dk_acc[rows, :].astype(jnp.bfloat16)
                dkv[b, :, head_size:] = dv_acc[rows, :].astype(jnp.bfloat16)

        return carry

    lax.fori_loop(0, (count + GROUP - 1) // GROUP, group_step, 0)
    for h in range(heads):
        dq_own[h] = dq_acc[h]
        dq_oth[h] = dq_acc[heads + h].astype(jnp.bfloat16)


def local_grads(span, block_docs, q_own, q_oth, g_own, g_oth, stat_own, stat_oth, docs, keys, values, interpret=False):
    tok, width = q_own.shape
    blocks, half_rows, head_size = keys.shape
    heads = width // head_size
    smem = pl.BlockSpec(memory_space=pltpu.SMEM)
    vmem = pl.BlockSpec(memory_space=pltpu.VMEM)
    rows = GROUP * half_rows
    return pl.pallas_call(
        functools.partial(grad_kernel, heads=heads, head_size=head_size),
        in_specs=[smem, smem] + [vmem] * 9,
        out_specs=[vmem] * 3,
        out_shape=[
            jax.ShapeDtypeStruct((heads, head_size, tok), jnp.float32),
            jax.ShapeDtypeStruct((heads, head_size, tok), jnp.bfloat16),
            jax.ShapeDtypeStruct((blocks, half_rows, 2 * head_size), jnp.bfloat16),
        ],
        scratch_shapes=[
            pltpu.VMEM((DOC_SLOTS, 2 * heads, tok), jnp.float32),
            pltpu.VMEM((2 * heads, head_size, tok), jnp.float32),
            pltpu.VMEM((rows, head_size), jnp.bfloat16),
            pltpu.VMEM((rows, head_size), jnp.bfloat16),
            pltpu.VMEM((head_size, rows), jnp.bfloat16),
            pltpu.VMEM((rows, head_size), jnp.float32),
            pltpu.VMEM((rows, head_size), jnp.float32),
            pltpu.SMEM((blocks + GROUP,), jnp.int32),
            pltpu.SMEM((blocks + GROUP,), jnp.int32),
        ],
        compiler_params=pltpu.CompilerParams(vmem_limit_bytes=40 << 20),
        interpret=interpret,
    )(span, block_docs, q_own, q_oth, g_own, g_oth, stat_own, stat_oth, docs, keys, values)


def body(queries, keys, values, outputs, out_grad, lse, doc_ids, image_docs):
    cores = lax.axis_size("c")
    owners = lax.axis_size("x") * lax.axis_size("yh")
    core = lax.axis_index("c")
    group_of = lax.axis_index(("x", "yh"))
    tok = queries.shape[0]
    heads = lse.shape[1]
    head_size = queries.shape[1] // heads
    block_rows = keys.shape[0]
    piece = block_rows // (owners * cores)
    half_rows = block_rows // cores
    swap = [(i, cores - 1 - i) for i in range(cores)]

    def mine(a):
        four = a.reshape(owners, cores, piece, a.shape[1])
        return lax.dynamic_slice(
            four, (0, core, 0, group_of * head_size), (owners, 1, piece, head_size)
        ).reshape(half_rows, head_size)

    both = jnp.concatenate([mine(keys), mine(values)], axis=1)
    plane = lax.all_gather(both, "yl", axis=0, tiled=True)
    key_all = lax.all_gather(plane[:, :head_size], "z", axis=0, tiled=True)
    value_all = lax.all_gather(plane[:, head_size:], "z", axis=0, tiled=True)

    delta = jnp.sum(
        out_grad.reshape(tok, heads, head_size).astype(jnp.float32)
        * outputs.reshape(tok, heads, head_size).astype(jnp.float32),
        axis=2,
    )
    stat_own = jnp.concatenate([delta, lse], axis=1).T
    q_oth = lax.ppermute(queries, "c", swap)
    g_oth = lax.ppermute(out_grad, "c", swap)
    stat_oth = lax.ppermute(stat_own, "c", swap)

    span = jnp.stack([doc_ids[0], doc_ids[tok - 1]])
    dq_own, dq_oth, dkv = local_grads(
        span, image_docs, queries, q_oth, out_grad, g_oth, stat_own, stat_oth, doc_ids[None, :],
        key_all.reshape(-1, half_rows, head_size), value_all.reshape(-1, half_rows, head_size),
    )
    dq_back = lax.ppermute(dq_oth, "c", swap)
    parts = lax.all_to_all(dkv, BLK, 0, 0, tiled=True)
    home = jnp.sum(parts.astype(jnp.float32), axis=0).astype(jnp.bfloat16)
    shares = lax.all_to_all(home.reshape(owners, piece, 2 * head_size), ("x", "yh"), 0, 0, tiled=True)
    kv_grad = jnp.transpose(shares, (1, 0, 2)).reshape(piece, owners * 2 * head_size)
    dquery = (dq_own + dq_back.astype(jnp.float32)).astype(jnp.bfloat16)
    query_grad = jnp.transpose(dquery, (2, 0, 1)).reshape(tok, heads * head_size)
    return (query_grad, kv_grad)


def solution(mesh):
    torus = Mesh(mesh.devices.reshape(12, 4, 4, 2, 2), BLK + PATCH)
    placed = (
        P(BLK, PATCH),
        P(BLK, None),
        P(BLK, None),
        P(BLK, PATCH),
        P(BLK, PATCH),
        P(BLK, PATCH),
        P(BLK),
        P(),
    )
    return jax.shard_map(
        body,
        mesh=torus,
        in_specs=placed,
        out_specs=(P(BLK, PATCH), P(BLK + PATCH, None)),
        check_vma=False,
    )
```

time: 710 us -> 182 us (0.26)
  the two profiles are of different devices: /device:TPU:1 before, /device:TPU:16 now
where the time goes in v1:
time: 182 us; the launch traced here: 180 us
  blocking collectives  72.2 us (40%)
  waiting for transfers between devices  51.9 us (29%)
  starting transfers between devices  36.5 us (20%)
  Pallas kernels  9.17 us (5%)
  other arithmetic  5.4 us (3%)
  local copies, waits for them, and re-layouts  4.25 us (2%)
    all_to_all x1, waiting for transfers between devices, body(): parts = lax.all_to_all(dkv, BLK, 0, 0, tiled=True)  43.9 us
    all_gather x1, blocking collectives, body(): value_all = lax.all_gather(plane[:, head_size:], 'z', axis=0, tiled=True)  27.6 us
    all_gather x1, blocking collectives, body(): key_all = lax.all_gather(plane[:, :head_size], 'z', axis=0, tiled=True)  24.1 us
    all_to_all x1, starting transfers between devices, body(): parts = lax.all_to_all(dkv, BLK, 0, 0, tiled=True)  21.4 us
    all_gather x1, blocking collectives, body(): plane = lax.all_gather(both, 'yl', axis=0, tiled=True)  20.5 us
    pallas_call x1, Pallas kernels, local_grads(): pl.pallas_call(functools.partial(grad_kernel, heads=heads, head_size=head...  9.17 us
    all_to_all x1, waiting for transfers between devices, body(): lax.all_to_all(home.reshape(owners, piece, 2 * head_size), ('x', 'yh'), 0...  7.95 us
    all_to_all x1, starting transfers between devices, body(): lax.all_to_all(home.reshape(owners, piece, 2 * head_size), ('x', 'yh'), 0...  6.75 us
  transfers between devices with their start and end apart: 6, of which 2 were waited for; matrix products, arithmetic and copies ran while one was open for 5% of the time, Pallas kernels for 0%

profile of v1, /device:TPU:16, one launch (start us, length us, event | category | flops | bytes accessed | tf_op | source)
XLA Modules:
  0.0 180.2 jit_solution(16002133786279679246)
XLA Ops:
  0.6 1.9 %collective-permute-start = (bf16[512,512]{1,0:T(8,128)(2,1)}, bf16[512,512]{1,0:T(8,128)(2,1)S(1)}, u32[]{:S(2)}, u32[]{:S(2)}) collective-permute-start(bf16[512,512]{1,0:T(8,128)(2,1)} %q_own.1), channel_id=1, source_target_pairs={{0,1},{1,0},{2,3},{3,2},{4,5},{5,4},{6,7},{7,6},{8,9},{9,8},{10,11... | collective-permute-start | bytes 1572872 | tf_op jit(solution)/shard_map/ppermute | solution.py:164
  2.6 2.4 %collective-permute-start.1 = (bf16[512,512]{1,0:T(8,128)(2,1)}, bf16[512,512]{1,0:T(8,128)(2,1)S(1)}, u32[]{:S(2)}, u32[]{:S(2)}) collective-permute-start(bf16[512,512]{1,0:T(8,128)(2,1)} %g_own.1), channel_id=1, source_target_pairs={{0,1},{1,0},{2,3},{3,2},{4,5},{5,4},{6,7},{7,6},{8,9},{9,8},{10,11... | collective-permute-start | bytes 1572872 | tf_op jit(solution)/shard_map/ppermute | solution.py:165
  5.0 1.3 convert_multiply_fusion
  6.3 0.0 copy-start.6
  6.3 0.4 mul.14
  6.7 0.0 copy-start.2
  6.7 0.6 reduce_sum.21
  7.3 0.0 copy-start
  7.4 0.0 copy-start.1
  7.4 0.0 copy-start.3
  7.4 0.1 copy.11
  7.5 0.0 copy-done.6
  7.5 2.1 %collective-permute-start.2 = (f32[8,512]{1,0:T(8,128)S(1)}, f32[8,512]{1,0:T(8,128)S(1)}, u32[]{:S(2)}, u32[]{:S(2)}) collective-permute-start(f32[8,512]{1,0:T(8,128)S(1)} %maximum_bitcast_fusion.stat_own), channel_id=1, source_target_pairs={{0,1},{1,0},{2,3},{3,2},{4,5},{5,4},{6,7},{7,6},{8,9},{9,8},{10,11... | collective-permute-start | bytes 49160 | tf_op jit(solution)/shard_map/ppermute | solution.py:166
  9.6 0.7 dynamic-slice_bitcast_fusion
  10.3 20.5 %all_gather.9 = bf16[256,256]{1,0:T(8,128)(2,1)S(1)} all-gather(bf16[64,256]{1,0:T(8,128)(2,1)S(1)} %pad_maximum_fusion), channel_id=1, replica_groups=mesh['z'=12,'yl'=4,'x'=4,'yh'=2,'c'=2] {'yl'}, dimensions={0}, use_global_device_ids=true | all-gather | bytes 163840 | tf_op jit(solution)/shard_map/all_gather | solution.py:154
  30.8 27.6 %all_gather.11 = bf16[3072,128]{1,0:T(8,128)(2,1)S(1)} all-gather(bf16[256,128]{1,0:T(8,128)(2,1)S(1)} %get-tuple-element.12), channel_id=1, replica_groups=mesh['z'=12,'yl'=4,'x'=4,'yh'=2,'c'=2] {'z'}, dimensions={0}, use_global_device_ids=true | all-gather | bytes 851968 | tf_op jit(solution)/shard_map/all_gather | solution.py:156
  58.4 0.0 copy-done.2
  58.4 0.6 fusion.1
  59.0 24.1 %all_gather.10 = bf16[3072,128]{1,0:T(8,128)(2,1)S(1)} all-gather(bf16[256,128]{1,0:T(8,128)(2,1)S(1)} %get-tuple-element.13), channel_id=1, replica_groups=mesh['z'=12,'yl'=4,'x'=4,'yh'=2,'c'=2] {'z'}, dimensions={0}, use_global_device_ids=true | all-gather | bytes 851968 | tf_op jit(solution)/shard_map/all_gather | solution.py:155
  83.2 1.4 pad_add_fusion.span
  84.5 0.0 collective-permute-done.2.stat_oth
  84.5 0.0 collective-permute-done.q_oth
  84.5 0.0 collective-permute-done.1.g_oth
  84.5 0.0 copy-done
  84.5 0.0 copy-done.1
  84.6 0.0 copy-done.3
  84.6 9.2 %shard_map.95 = (f32[4,128,512]{2,1,0:T(8,128)S(1)}, bf16[4,128,512]{2,1,0:T(8,128)(2,1)S(1)}, bf16[48,64,256]{2,1,0:T(8,128)(2,1)}) custom-call(s32[2]{0:T(128)S(1)} %pad_add_fusion.span, s32[48]{0:T(128)S(1)} %copy-done.3, bf16[512,512]{1,0:T(8,128)(2,1)S(1)} %copy-done.1, bf16[512,512]{1,0:T(8,128)(2,1)S(1)} %collective-permute-done.q_oth, ...), custom_call_target="tpu_custom_call" | custom-call | tf_op jit(solution)/shard_map/pallas_call | solution.py:109
  93.7 0.0 copy-start.4
  93.7 0.8 copy-done.4
  94.5 0.0 copy-start.5
  94.5 21.4 %all-to-all-start = ((bf16[48,64,256]{2,1,0:T(8,128)(2,1)}), bf16[48,64,256]{2,1,0:T(8,128)(2,1)S(1)}, u32[]{:S(2)}, u32[]{:S(2)}) async-start(bf16[48,64,256]{2,1,0:T(8,128)(2,1)} %get-tuple-element.7), calls=%async_computation | async-start | bytes 3145728 | tf_op jit(solution)/shard_map/all_to_all | solution.py:174
  115.9 0.0 copy-done.5
  115.9 1.9 %collective-permute-start.3 = (bf16[4,128,512]{2,1,0:T(8,128)(2,1)S(1)}, bf16[4,128,512]{2,1,0:T(8,128)(2,1)}, u32[]{:S(2)}, u32[]{:S(2)}) collective-permute-start(bf16[4,128,512]{2,1,0:T(8,128)(2,1)S(1)} %copy-done.5), channel_id=1, source_target_pairs={{0,1},{1,0},{2,3},{3,2},{4,5},{5,4},{6,7},{7,6},{8,9},{9,8},{10,11... | collective-permute-start | bytes 1572872 | tf_op jit(solution)/shard_map/ppermute | solution.py:173
  117.9 43.9 %all-to-all-done = bf16[48,64,256]{2,1,0:T(8,128)(2,1)S(1)} async-done(((bf16[48,64,256]{2,1,0:T(8,128)(2,1)}), bf16[48,64,256]{2,1,0:T(8,128)(2,1)S(1)}, u32[]{:S(2)}, u32[]{:S(2)}) %all-to-all-start) | async-done | bytes 1572896 | tf_op jit(solution)/shard_map/all_to_all | solution.py:174
  161.8 0.8 reduce_sum.22
  162.6 6.8 %all-to-all-start.1 = ((bf16[8,8,256]{2,1,0:T(8,128)(2,1)}), bf16[8,8,256]{2,1,0:T(8,128)(2,1)S(1)}, u32[]{:S(2)}, u32[]{:S(2)}) async-start(bf16[8,8,256]{2,1,0:T(8,128)(2,1)} %bitcast.10), calls=%async_computation.1 | async-start | bytes 65536 | tf_op jit(solution)/shard_map/all_to_all | solution.py:176
  169.4 0.0 collective-permute-done.3
  169.4 1.2 add_convert_fusion
  170.6 1.0 copy.12
  171.6 7.9 %all-to-all-done.1 = bf16[8,8,256]{2,1,0:T(8,128)(2,1)S(1)} async-done(((bf16[8,8,256]{2,1,0:T(8,128)(2,1)}), bf16[8,8,256]{2,1,0:T(8,128)(2,1)S(1)}, u32[]{:S(2)}, u32[]{:S(2)}) %all-to-all-start.1) | async-done | bytes 32800 | tf_op jit(solution)/shard_map/all_to_all | solution.py:176
  179.6 0.6 copy.14
  (3 shorter events, 0.0 us)
Async XLA Ops:
  0.6 83.9 %collective-permute-start = (bf16[512,512]{1,0:T(8,128)(2,1)}, bf16[512,512]{1,0:T(8,128)(2,1)S(1)}, u32[]{:S(2)}, u32[]{:S(2)}) collective-permute-start(bf16[512,512]{1,0:T(8,128)(2,1)} %q_own.1), channel_id=1, source_target_pairs={{0,1},{1,0},{2,3},{3,2},{4,5},{5,4},{6,7},{7,6},{8,9},{9,8},{10,11... | collective-permute-start | bytes 1572872 | tf_op jit(solution)/shard_map/ppermute | solution.py:164
  2.6 82.0 %collective-permute-start.1 = (bf16[512,512]{1,0:T(8,128)(2,1)}, bf16[512,512]{1,0:T(8,128)(2,1)S(1)}, u32[]{:S(2)}, u32[]{:S(2)}) collective-permute-start(bf16[512,512]{1,0:T(8,128)(2,1)} %g_own.1), channel_id=1, source_target_pairs={{0,1},{1,0},{2,3},{3,2},{4,5},{5,4},{6,7},{7,6},{8,9},{9,8},{10,11... | collective-permute-start | bytes 1572872 | tf_op jit(solution)/shard_map/ppermute | solution.py:165
  6.3 1.2 copy-start.6
  6.7 51.7 %copy-start.2 = (s32[512]{0:T(512)S(1)}, s32[512]{0:T(512)}, u32[]{:S(2)}) copy-start(s32[512]{0:T(512)} %param.14) | copy-start | bytes 6148
  7.3 77.2 %copy-start = (bf16[512,512]{1,0:T(8,128)(2,1)S(1)}, bf16[512,512]{1,0:T(8,128)(2,1)}, u32[]{:S(2)}) copy-start(bf16[512,512]{1,0:T(8,128)(2,1)} %g_own.1) | copy-start | bytes 1572868
  7.4 77.2 %copy-start.1 = (bf16[512,512]{1,0:T(8,128)(2,1)S(1)}, bf16[512,512]{1,0:T(8,128)(2,1)}, u32[]{:S(2)}) copy-start(bf16[512,512]{1,0:T(8,128)(2,1)} %q_own.1) | copy-start | bytes 1572868
  7.4 77.2 %copy-start.3 = (s32[48]{0:T(128)S(1)}, s32[48]{0:T(128)}, u32[]{:S(2)}) copy-start(s32[48]{0:T(128)} %block_docs.1) | copy-start | bytes 580
  7.5 77.0 %collective-permute-start.2 = (f32[8,512]{1,0:T(8,128)S(1)}, f32[8,512]{1,0:T(8,128)S(1)}, u32[]{:S(2)}, u32[]{:S(2)}) collective-permute-start(f32[8,512]{1,0:T(8,128)S(1)} %maximum_bitcast_fusion.stat_own), channel_id=1, source_target_pairs={{0,1},{1,0},{2,3},{3,2},{4,5},{5,4},{6,7},{7,6},{8,9},{9,8},{10,11... | collective-permute-start | bytes 49160 | tf_op jit(solution)/shard_map/ppermute | solution.py:166
  93.7 0.8 copy-start.4
  94.5 21.4 %copy-start.5 = (bf16[4,128,512]{2,1,0:T(8,128)(2,1)S(1)}, bf16[4,128,512]{2,1,0:T(8,128)(2,1)}, u32[]{:S(2)}) copy-start(bf16[4,128,512]{2,1,0:T(8,128)(2,1)} %copy-done.4) | copy-start | bytes 1572868
  94.5 67.3 %all-to-all-start = ((bf16[48,64,256]{2,1,0:T(8,128)(2,1)}), bf16[48,64,256]{2,1,0:T(8,128)(2,1)S(1)}, u32[]{:S(2)}, u32[]{:S(2)}) async-start(bf16[48,64,256]{2,1,0:T(8,128)(2,1)} %get-tuple-element.7), calls=%async_computation | async-start | bytes 3145728 | tf_op jit(solution)/shard_map/all_to_all | solution.py:174
  115.9 53.4 %collective-permute-start.3 = (bf16[4,128,512]{2,1,0:T(8,128)(2,1)S(1)}, bf16[4,128,512]{2,1,0:T(8,128)(2,1)}, u32[]{:S(2)}, u32[]{:S(2)}) collective-permute-start(bf16[4,128,512]{2,1,0:T(8,128)(2,1)S(1)} %copy-done.5), channel_id=1, source_target_pairs={{0,1},{1,0},{2,3},{3,2},{4,5},{5,4},{6,7},{7,6},{8,9},{9,8},{10,11... | collective-permute-start | bytes 1572872 | tf_op jit(solution)/shard_map/ppermute | solution.py:173
  162.6 16.9 %all-to-all-start.1 = ((bf16[8,8,256]{2,1,0:T(8,128)(2,1)}), bf16[8,8,256]{2,1,0:T(8,128)(2,1)S(1)}, u32[]{:S(2)}, u32[]{:S(2)}) async-start(bf16[8,8,256]{2,1,0:T(8,128)(2,1)} %bitcast.10), calls=%async_computation.1 | async-start | bytes 65536 | tf_op jit(solution)/shard_map/all_to_all | solution.py:176

commit v2 on v1

v2 whole, which is shorter than its diff:
```python
import functools
import math

import jax
import jax.numpy as jnp
from jax import lax
from jax.experimental import pallas as pl
from jax.experimental.pallas import tpu as pltpu
from jax.sharding import Mesh
from jax.sharding import PartitionSpec as P

BLK = ("z", "yl")
PATCH = ("x", "yh", "c")
DOC_SLOTS = 8
PAD_DOC = 7
GROUP = 4
CHUNK = 256
MASKED = 1e30
SLOTS = 28
INFO_ROWS = 16
PIECES = 2


def dot_nt(a, b):
    return lax.dot_general(a, b, (((1,), (1,)), ((), ())), preferred_element_type=jnp.float32)


def dot_nn(a, b):
    return lax.dot_general(a, b, (((1,), (0,)), ((), ())), preferred_element_type=jnp.float32)


def ready_kernel(doc_ids, block_docs, where, keys, values, outputs, grads, lse, both, stats, table, order, tally,
                 *, owners, cores, cols, heads, head_size):
    blocks = block_docs.shape[0]
    block_rows = keys.shape[0]
    tok = grads.shape[0]
    half_rows = block_rows // cores
    piece = half_rows // (owners * cols)
    core, group = where[0], where[1]

    for d in range(DOC_SLOTS + 1):
        tally[d] = 0

    def count_one(b, carry):
        slot = block_docs[b] + 1
        tally[slot] = tally[slot] + 1
        return carry

    lax.fori_loop(0, blocks, count_one, 0)
    for d in range(1, DOC_SLOTS + 1):
        tally[d] = tally[d] + tally[d - 1]
    first = tally[doc_ids[0]]
    count = tally[doc_ids[tok - 1] + 1] - first

    def place(b, carry):
        doc = block_docs[b]
        at = tally[doc]
        tally[doc] = at + 1
        table[b] = at
        order[at] = b
        return carry

    lax.fori_loop(0, blocks, place, 0)
    order[blocks] = first
    order[blocks + 1] = count

    at = lax.broadcasted_iota(jnp.int32, (half_rows, block_rows), 0)
    row = lax.broadcasted_iota(jnp.int32, (half_rows, block_rows), 1)
    col, owner, sub = at // (owners * piece), at // piece % owners, at % piece
    pick = (row == ((owner * cores + core) * cols + col) * piece + sub).astype(jnp.float32).astype(jnp.bfloat16)
    lanes = pl.ds(pl.multiple_of(group * head_size, head_size), head_size)
    both[:half_rows, :head_size] = dot_nn(pick, keys[:, lanes]).astype(jnp.bfloat16)
    both[:half_rows, head_size:] = dot_nn(pick, values[:, lanes]).astype(jnp.bfloat16)
    lane = lax.broadcasted_iota(jnp.int32, (INFO_ROWS, 2 * head_size), 1)
    info = jnp.where(lane == 0, first, jnp.where(lane == 1, count, 0))
    both[half_rows:, :] = info.astype(jnp.float32).astype(jnp.bfloat16)

    lane = lax.broadcasted_iota(jnp.int32, (tok, head_size), 1)
    wide = jnp.zeros((tok, head_size), jnp.float32)
    for h in range(heads):
        span = slice(h * head_size, (h + 1) * head_size)
        product = grads[:, span].astype(jnp.float32) * outputs[:, span].astype(jnp.float32)
        wide = jnp.where(lane == h, jnp.sum(product, axis=1, keepdims=True), wide)
    stats[:heads, :] = wide.T[:heads, :]
    stats[heads:, :] = lse[...]


def ready(doc_ids, block_docs, where, keys, values, outputs, grads, lse, owners, cores, cols, interpret=False):
    heads, tok = lse.shape
    head_size = grads.shape[1] // heads
    blocks = block_docs.shape[0]
    half_rows = keys.shape[0] // cores
    smem = pl.BlockSpec(memory_space=pltpu.SMEM)
    vmem = pl.BlockSpec(memory_space=pltpu.VMEM)
    return pl.pallas_call(
        functools.partial(
            ready_kernel, owners=owners, cores=cores, cols=cols, heads=heads, head_size=head_size
        ),
        in_specs=[smem] * 3 + [vmem] * 5,
        out_specs=[vmem] * 2 + [smem] * 2,
        out_shape=[
            jax.ShapeDtypeStruct((half_rows + INFO_ROWS, 2 * head_size), jnp.bfloat16),
            jax.ShapeDtypeStruct((2 * heads, tok), jnp.float32),
            jax.ShapeDtypeStruct((blocks,), jnp.int32),
            jax.ShapeDtypeStruct((blocks + 2,), jnp.int32),
        ],
        scratch_shapes=[pltpu.SMEM((DOC_SLOTS + 1,), jnp.int32)],
        compiler_params=pltpu.CompilerParams(vmem_limit_bytes=12 << 20),
        interpret=interpret,
    )(doc_ids, block_docs, where, keys, values, outputs, grads, lse)


def grad_kernel(doc_ids, block_docs, order, plane, q_own, q_oth, g_own, g_oth, stat_own, stat_oth, docs, *refs,
                heads, head_size, half_rows, pieces):
    gathered, refs = refs[:pieces], refs[pieces:]
    dq_own, dq_oth, pack, rest, near, lse_doc, dq_acc, k_grp, v_grp, kt_grp, dk_acc, dv_acc = refs
    blocks = block_docs.shape[0]
    tile = half_rows + INFO_ROWS
    cols, piece_rows, _ = gathered[0].shape
    piece_planes = piece_rows // tile
    tok = docs.shape[1]
    part = half_rows // cols
    scaling = head_size ** (-0.5)
    log2e = math.log2(math.e)
    first, count = order[blocks], order[blocks + 1]

    lane = lax.broadcasted_iota(jnp.int32, (INFO_ROWS, head_size), 1)
    most = jnp.zeros((INFO_ROWS, head_size), jnp.float32)
    for col in range(cols):
        mate = jnp.zeros((INFO_ROWS, head_size), jnp.float32)
        for p, ref in enumerate(gathered):
            for z in range(piece_planes):
                info = ref[col, z * tile + half_rows:(z + 1) * tile, :head_size].astype(jnp.float32)
                most = jnp.maximum(most, info)
                mate = jnp.where(plane[0] == p * piece_planes + z, info, mate)
        near[col] = jnp.max(jnp.where(lane == 0, mate, 0.0)).astype(jnp.int32)
        near[cols + col] = jnp.max(jnp.where(lane == 1, mate, 0.0)).astype(jnp.int32)
    near[2 * cols] = jnp.max(jnp.where(lane == 1, most, 0.0)).astype(jnp.int32)

    doc_row = docs[...]
    for d in range(DOC_SLOTS):
        inside = doc_row == d
        for s, stat in enumerate((stat_own, stat_oth)):
            lse_doc[d, s * heads:(s + 1) * heads, :] = jnp.where(inside, stat[heads:, :] * log2e, MASKED)
    dq_acc[...] = jnp.zeros_like(dq_acc)
    pack[...] = jnp.zeros_like(pack)
    rest[...] = jnp.zeros_like(rest)

    def group_step(grp, carry):
        base = grp * GROUP
        group_docs = []
        for s in range(GROUP):
            b = order[first + jnp.minimum(base + s, count - 1)]
            col, at = lax.rem(b, cols), lax.div(b, cols)
            block = gathered[0][col, pl.ds(pl.multiple_of(jnp.minimum(at, piece_planes - 1) * tile, 16), half_rows), :]
            for p in range(1, pieces):
                near_at = jnp.clip(at - p * piece_planes, 0, piece_planes - 1)
                other = gathered[p][col, pl.ds(pl.multiple_of(near_at * tile, 16), half_rows), :]
                block = jnp.where(at >= p * piece_planes, other, block)
            k_grp[s * half_rows:(s + 1) * half_rows, :] = block[:, :head_size]
            v_grp[s * half_rows:(s + 1) * half_rows, :] = block[:, head_size:]
            group_docs.append(block_docs[b])
        slot_docs = [jnp.where(base + s < count, group_docs[s], PAD_DOC) for s in range(GROUP)]
        kt_grp[...] = k_grp[...].T
        dk_acc[...] = jnp.zeros_like(dk_acc)
        dv_acc[...] = jnp.zeros_like(dv_acc)
        for start in range(0, tok, CHUNK):
            toks = slice(start, start + CHUNK)

            @pl.when((group_docs[0] <= doc_ids[start + CHUNK - 1]) & (group_docs[-1] >= doc_ids[start]))
            def _():
                for h in range(2 * heads):
                    q_ref, g_ref, stat = (q_own, g_own, stat_own) if h < heads else (q_oth, g_oth, stat_oth)
                    at = (h % heads) * head_size
                    query = q_ref[toks, at:at + head_size]
                    grad = g_ref[toks, at:at + head_size]
                    delta = stat[h % heads:h % heads + 1, toks]
                    score = dot_nt(k_grp[...], query)
                    dprob = dot_nt(v_grp[...], grad)
                    probs, dscores = [], []
                    for s in range(GROUP):
                        rows = slice(s * half_rows, (s + 1) * half_rows)
                        stats = lse_doc[slot_docs[s], h:h + 1, toks]
                        prob = jnp.exp2(score[rows] * (scaling * log2e) - stats)
                        probs.append(prob.astype(jnp.bfloat16))
                        dscores.append((prob * (dprob[rows] - delta) * scaling).astype(jnp.bfloat16))
                    prob_low = jnp.concatenate(probs, axis=0)
                    dscore = jnp.concatenate(dscores, axis=0)
                    dk_acc[...] += dot_nn(dscore, query)
                    dv_acc[...] += dot_nn(prob_low, grad)
                    dq_acc[h, :, toks] += dot_nn(kt_grp[...], dscore)

        def put(out, slot):
            for s in range(GROUP):
                for j in range(cols):
                    rows = slice(s * half_rows + j * part, s * half_rows + (j + 1) * part)
                    out[j, slot + s, :, :head_size] = dk_acc[rows, :].astype(jnp.bfloat16)
                    out[j, slot + s, :, head_size:] = dv_acc[rows, :].astype(jnp.bfloat16)

        @pl.when(base < SLOTS)
        def _():
            put(pack, jnp.minimum(base, SLOTS - GROUP))

        @pl.when(base >= SLOTS)
        def _():
            put(rest, jnp.maximum(base - SLOTS, 0))

        return carry

    lax.fori_loop(0, (count + GROUP - 1) // GROUP, group_step, 0)
    for h in range(heads):
        dq_own[h] = dq_acc[h]
        dq_oth[h] = dq_acc[heads + h].astype(jnp.bfloat16)


def local_grads(doc_ids, block_docs, order, plane, q_own, q_oth, g_own, g_oth, stat_own, stat_oth, gathered, half_rows,
                interpret=False):
    tok, width = q_own.shape
    cols = gathered[0].shape[0]
    head_size = gathered[0].shape[2] // 2
    blocks = block_docs.shape[0]
    heads = width // head_size
    smem = pl.BlockSpec(memory_space=pltpu.SMEM)
    vmem = pl.BlockSpec(memory_space=pltpu.VMEM)
    rows = GROUP * half_rows
    return pl.pallas_call(
        functools.partial(grad_kernel, heads=heads, head_size=head_size, half_rows=half_rows, pieces=len(gathered)),
        in_specs=[smem] * 4 + [vmem] * (7 + len(gathered)),
        out_specs=[vmem] * 4 + [smem],
        out_shape=[
            jax.ShapeDtypeStruct((heads, head_size, tok), jnp.float32),
            jax.ShapeDtypeStruct((heads, head_size, tok), jnp.bfloat16),
            jax.ShapeDtypeStruct((cols, SLOTS, half_rows // cols, 2 * head_size), jnp.bfloat16),
            jax.ShapeDtypeStruct((cols, blocks - SLOTS, half_rows // cols, 2 * head_size), jnp.bfloat16),
            jax.ShapeDtypeStruct((2 * cols + 1,), jnp.int32),
        ],
        scratch_shapes=[
            pltpu.VMEM((DOC_SLOTS, 2 * heads, tok), jnp.float32),
            pltpu.VMEM((2 * heads, head_size, tok), jnp.float32),
            pltpu.VMEM((rows, head_size), jnp.bfloat16),
            pltpu.VMEM((rows, head_size), jnp.bfloat16),
            pltpu.VMEM((head_size, rows), jnp.bfloat16),
            pltpu.VMEM((rows, head_size), jnp.float32),
            pltpu.VMEM((rows, head_size), jnp.float32),
        ],
        compiler_params=pltpu.CompilerParams(vmem_limit_bytes=24 << 20),
        interpret=interpret,
    )(doc_ids, block_docs, order, plane, q_own, q_oth, g_own, g_oth, stat_own, stat_oth, doc_ids[None, :], *gathered)


def spread_kernel(table, near, *refs, blocks):
    pieces, out = refs[:-1], refs[-1]
    cols = pieces[0].shape[0]

    def step(b, carry):
        total = jnp.zeros(out.shape[1:], jnp.float32)
        for i in range(cols):
            slot = table[b] - near[i]
            begin = 0
            for piece in pieces:
                size = piece.shape[1]
                here = (slot >= begin) & (slot < jnp.minimum(near[cols + i], begin + size))
                part = piece[i, jnp.clip(slot - begin, 0, size - 1)].astype(jnp.float32)
                total = total + jnp.where(here, part, 0.0)
                begin += size
        out[b] = total.astype(jnp.bfloat16)
        return carry

    lax.fori_loop(0, blocks, step, 0, unroll=4)


def spread(table, near, pieces, blocks, interpret=False):
    smem = pl.BlockSpec(memory_space=pltpu.SMEM)
    vmem = pl.BlockSpec(memory_space=pltpu.VMEM)
    return pl.pallas_call(
        functools.partial(spread_kernel, blocks=blocks),
        in_specs=[smem] * 2 + [vmem] * len(pieces),
        out_specs=vmem,
        out_shape=jax.ShapeDtypeStruct((blocks,) + pieces[0].shape[2:], jnp.bfloat16),
        compiler_params=pltpu.CompilerParams(vmem_limit_bytes=12 << 20),
        interpret=interpret,
    )(table, near, *pieces)


def body(queries, keys, values, outputs, out_grad, lse, doc_ids, image_docs):
    cores = lax.axis_size("c")
    cols = lax.axis_size("yl")
    planes = lax.axis_size("z")
    owners = lax.axis_size("x") * lax.axis_size("yh")
    tok = queries.shape[0]
    heads = lse.shape[1]
    head_size = queries.shape[1] // heads
    blocks = image_docs.shape[0]
    half_rows = keys.shape[0] // cores
    piece = half_rows // (owners * cols)
    swap = [(i, cores - 1 - i) for i in range(cores)]

    where = jnp.stack([lax.axis_index("c"), lax.axis_index(("x", "yh"))]).astype(jnp.int32)
    both, stat_own, table, order = ready(
        doc_ids, image_docs, where, keys, values, outputs, out_grad, lse.T, owners, cores, cols
    )
    q_oth = lax.ppermute(queries, "c", swap)
    g_oth = lax.ppermute(out_grad, "c", swap)
    stat_oth = lax.ppermute(stat_own, "c", swap)

    column = lax.all_gather(both, "z", axis=0, tiled=True)
    cut = column.shape[0] // PIECES
    gathered = [lax.all_gather(column[p * cut:(p + 1) * cut], "yl", axis=0) for p in range(PIECES)]

    plane = lax.axis_index("z").astype(jnp.int32).reshape(1)
    dq_own, dq_oth, pack, rest, near = local_grads(
        doc_ids, image_docs, order, plane, queries, q_oth, out_grad, g_oth, stat_own, stat_oth, gathered, half_rows
    )
    dq_back = lax.ppermute(dq_oth, "c", swap)

    shared = lax.all_to_all(pack, "yl", 0, 0, tiled=True)

    def some(pieces):
        return spread(table, near, pieces[:1], blocks)

    def every(pieces):
        late = lax.all_to_all(pieces[1], "yl", 0, 0, tiled=True)
        return spread(table, near, (pieces[0], late), blocks)

    sums = lax.cond(near[2 * cols] <= SLOTS, some, every, (shared, rest))
    parts = lax.all_to_all(sums.reshape(planes, half_rows, 2 * head_size), "z", 0, 0, tiled=True)
    home = jnp.sum(parts.astype(jnp.float32), axis=0).astype(jnp.bfloat16)
    shares = lax.all_to_all(home.reshape(cols * owners, piece, 2 * head_size), ("yl", "x", "yh"), 0, 0, tiled=True)
    kv_grad = jnp.transpose(shares.reshape(cols, owners, piece, 2 * head_size), (0, 2, 1, 3)).reshape(
        cols * piece, owners * 2 * head_size
    )
    dquery = (dq_own + dq_back.astype(jnp.float32)).astype(jnp.bfloat16)
    query_grad = jnp.transpose(dquery, (2, 0, 1)).reshape(tok, heads * head_size)
    return (query_grad, kv_grad)


def solution(mesh):
    torus = Mesh(mesh.devices.reshape(12, 4, 4, 2, 2), BLK + PATCH)
    placed = (
        P(BLK, PATCH),
        P(BLK, None),
        P(BLK, None),
        P(BLK, PATCH),
        P(BLK, PATCH),
        P(BLK, PATCH),
        P(BLK),
        P(),
    )
    return jax.shard_map(
        body,
        mesh=torus,
        in_specs=placed,
        out_specs=(P(BLK, PATCH), P(BLK + PATCH, None)),
        check_vma=False,
    )
```

time: 182 us -> 168 us (0.923)
  the two profiles are of different devices: /device:TPU:16 before, /device:TPU:8 now
where the time goes in v2:
time: 168 us; the launch traced here: 167 us
  blocking collectives  72.7 us (43%)
  waiting for transfers between devices  31.8 us (19%)
  starting transfers between devices  28.8 us (17%)
  Pallas kernels  19.6 us (12%)
  local copies, waits for them, and re-layouts  12.7 us (8%)
    all_gather x2, blocking collectives, body(): lax.all_gather(column[p * cut:(p + 1) * cut], 'yl', axis=0)  37.7 us
    all_gather x1, blocking collectives, body(): column = lax.all_gather(both, 'z', axis=0, tiled=True)  35 us
    pallas_call x1, Pallas kernels, local_grads(): pl.pallas_call(functools.partial(grad_kernel, heads=heads, head_size=head...  14.8 us
    all_to_all x1, waiting for transfers between devices, body(): lax.all_to_all(sums.reshape(planes, half_rows, 2 * head_size), 'z', 0, 0,...  14.3 us
    unnamed x36, local copies, waits for them, and re-layouts  11.5 us
    all_to_all x1, starting transfers between devices, body(): lax.all_to_all(home.reshape(cols * owners, piece, 2 * head_size), ('yl',...  11.3 us
    all_to_all x1, waiting for transfers between devices, body(): shared = lax.all_to_all(pack, 'yl', 0, 0, tiled=True)  9.79 us
    all_to_all x1, waiting for transfers between devices, body(): lax.all_to_all(home.reshape(cols * owners, piece, 2 * head_size), ('yl',...  7.66 us
  transfers between devices with their start and end apart: 7, of which 3 were waited for; matrix products, arithmetic and copies ran while one was open for 2% of the time, Pallas kernels for 2%

profile of v2, /device:TPU:8, one launch (start us, length us, event | category | flops | bytes accessed | tf_op | source)
XLA Modules:
  0.0 167.3 jit_solution(15321912833851647203)
XLA Ops:
  0.6 1.9 %collective-permute-start.1 = (bf16[512,512]{1,0:T(8,128)(2,1)}, bf16[512,512]{1,0:T(8,128)(2,1)S(1)}, u32[]{:S(2)}, u32[]{:S(2)}) collective-permute-start(bf16[512,512]{1,0:T(8,128)(2,1)} %g_own.1), channel_id=1, source_target_pairs={{0,1},{1,0},{2,3},{3,2},{4,5},{5,4},{6,7},{7,6},{8,9},{9,8},{10,11... | collective-permute-start | bytes 1572872 | tf_op jit(solution)/shard_map/ppermute | solution.py:303
  2.6 0.0 copy-start.11
  2.6 0.0 copy-start.10
  2.6 0.1 pad_add_fusion.where
  2.7 0.6 copy-done.11
  3.3 0.0 copy-done.10
  3.3 0.1 copy-done.12
  3.3 1.0 copy-done
  4.4 1.0 copy-done.3
  5.4 0.9 copy-done.8
  6.4 0.9 copy-done.9
  7.3 2.6 %shard_map.95 = (bf16[80,256]{1,0:T(8,128)(2,1)S(1)}, f32[8,512]{1,0:T(8,128)}, s32[48]{0:T(128)S(1)}, s32[50]{0:T(128)S(1)}) custom-call(s32[512]{0:T(512)S(1)} %copy-done.10, s32[48]{0:T(128)S(1)} %copy-done.12, s32[2]{0:T(128)S(1)} %pad_add_fusion.where, bf16[128,1024]{1,0:T(8,128)(2,1)S(1)} %copy-done.8, bf16[128,1024]{1,0:T(8,128)(2,1)S(1)} %copy-done.9, ...), custom_call_target="tpu_custom_call" | custom-call | tf_op jit(solution)/shard_map/pallas_call | solution.py:95
  9.9 2.4 %collective-permute-start.2 = (f32[8,512]{1,0:T(8,128)}, f32[8,512]{1,0:T(8,128)}, u32[]{:S(2)}, u32[]{:S(2)}) collective-permute-start(f32[8,512]{1,0:T(8,128)} %get-tuple-element.36.stat_own), channel_id=1, source_target_pairs={{0,1},{1,0},{2,3},{3,2},{4,5},{5,4},{6,7},{7,6},{8,9},{9,8},{10,11... | collective-permute-start | bytes 49160 | tf_op jit(solution)/shard_map/ppermute | solution.py:304
  12.4 0.0 copy-done.4
  12.4 1.9 %collective-permute-start = (bf16[512,512]{1,0:T(8,128)(2,1)S(1)}, bf16[512,512]{1,0:T(8,128)(2,1)}, u32[]{:S(2)}, u32[]{:S(2)}) collective-permute-start(bf16[512,512]{1,0:T(8,128)(2,1)S(1)} %copy-done.4), channel_id=1, source_target_pairs={{0,1},{1,0},{2,3},{3,2},{4,5},{5,4},{6,7},{7,6},{8,9},{9,8},{10,11... | collective-permute-start | bytes 1572872 | tf_op jit(solution)/shard_map/ppermute | solution.py:302
  14.3 35.0 %all_gather.15 = bf16[960,256]{1,0:T(8,128)(2,1)S(1)} all-gather(bf16[80,256]{1,0:T(8,128)(2,1)S(1)} %get-tuple-element.37), channel_id=1, replica_groups=mesh['z'=12,'yl'=4,'x'=4,'yh'=2,'c'=2] {'z'}, dimensions={0}, use_global_device_ids=true | all-gather | bytes 532480 | tf_op jit(solution)/shard_map/all_gather | solution.py:306
  49.3 19.1 %all-gather.1 = bf16[1920,256]{1,0:T(8,128)(2,1)S(1)} all-gather(bf16[480,256]{1,0:T(8,128)(2,1)S(1)} %get-tuple-element.50), channel_id=3, replica_groups=mesh['z'=12,'yl'=4,'x'=4,'yh'=2,'c'=2] {'yl'}, dimensions={0}, use_global_device_ids=true | all-gather | bytes 1228800 | tf_op jit(solution)/shard_map/all_gather | solution.py:308
  68.5 18.5 %all-gather = bf16[1920,256]{1,0:T(8,128)(2,1)S(1)} all-gather(bf16[480,256]{1,0:T(8,128)(2,1)S(1)} %get-tuple-element.51), channel_id=2, replica_groups=mesh['z'=12,'yl'=4,'x'=4,'yh'=2,'c'=2] {'yl'}, dimensions={0}, use_global_device_ids=true | all-gather | bytes 1228800 | tf_op jit(solution)/shard_map/all_gather | solution.py:308
  87.0 0.0 collective-permute-done.2.stat_oth
  87.0 0.0 collective-permute-done.q_oth
  87.0 0.0 collective-permute-done.1.g_oth
  87.0 0.0 copy-start.6
  87.0 0.8 copy-done.6
  87.8 0.0 copy-done.1
  87.8 1.0 copy-done.5
  88.8 1.0 copy-done.7
  89.9 14.8 %shard_map.96 = (f32[4,128,512]{2,1,0:T(8,128)S(1)}, bf16[4,128,512]{2,1,0:T(8,128)(2,1)S(1)}, bf16[4,28,16,256]{3,2,1,0:T(8,128)(2,1)S(1)}, bf16[4,20,16,256]{3,2,1,0:T(8,128)(2,1)}, s32[9]{0:T(128)}) custom-call(s32[512]{0:T(512)S(1)} %copy-done.10, s32[48]{0:T(128)S(1)} %copy-done.12, s32[50]{0:T(128)S(1)} %get-tuple-element.35.order, s32[1]{0:T(128)} %bitcast.3.plane, ...), custom_call_target="tpu_custom_call" | custom-call | tf_op jit(solution)/shard_map/pallas_call | solution.py:226
  104.7 0.0 copy-start.2
  104.7 0.9 copy-done.2
  105.7 0.8 copy-done.13
  106.5 5.5 %all-to-all-start.1 = ((bf16[4,28,16,256]{3,2,1,0:T(8,128)(2,1)}), bf16[4,28,16,256]{3,2,1,0:T(8,128)(2,1)S(1)}, u32[]{:S(2)}, u32[]{:S(2)}) async-start(bf16[4,28,16,256]{3,2,1,0:T(8,128)(2,1)} %copy-done.2), calls=%async_computation.1 | async-start | bytes 1835008 | tf_op jit(solution)/shard_map/all_to_all | solution.py:316
  112.0 0.6 copy-done.16
  112.6 0.6 slice.11
  113.8 9.8 %all-to-all-done.1 = bf16[4,28,16,256]{3,2,1,0:T(8,128)(2,1)S(1)} async-done(((bf16[4,28,16,256]{3,2,1,0:T(8,128)(2,1)}), bf16[4,28,16,256]{3,2,1,0:T(8,128)(2,1)S(1)}, u32[]{:S(2)}, u32[]{:S(2)}) %all-to-all-start.1) | async-done | bytes 917536 | tf_op jit(solution)/shard_map/all_to_all | solution.py:316
  123.6 0.0 copy-done.15
  123.6 2.1 %conditional.1 = (bf16[48,16,256]{2,1,0:T(8,128)(2,1)}) conditional(s32[]{:T(128)} %bitcast.9, (bf16[4,20,16,256]{3,2,1,0:T(8,128)(2,1)S(1)}, s32[48]{0:T(128)S(1)}, s32[9]{0:T(128)S(1)}, bf16[4,28,16,256]{3,2,1,0:T(8,128)(2,1)S(1)}) %tuple.24, (s32[48]{0:T(128)S(1)}, s32[9]{0:T(128)S(1)}, bf16[4,28,16,256]{3,2,1,0:T(8,128)(2,1)S(1)}) %tuple.25), branch_computations={%region_0.0_spmd, %region_1.0_spmd} | conditional | bytes 1310728 | solution.py:325
  123.6 2.1 %branch_1_fun.1 = bf16[48,16,256]{2,1,0:T(8,128)(2,1)} custom-call(s32[48]{0:T(128)S(1)} %get-tuple-element.21.table, s32[9]{0:T(128)S(1)} %get-tuple-element.22.near, bf16[4,28,16,256]{3,2,1,0:T(8,128)(2,1)S(1)} %get-tuple-element.23.refs_0_), custom_call_target="tpu_custom_call" | custom-call | tf_op jit(solution)/shard_map/cond/branch_1_fun/pallas_call | solution.py:275
  125.8 3.7 %all-to-all-start.2 = ((bf16[12,64,256]{2,1,0:T(8,128)(2,1)}), bf16[12,64,256]{2,1,0:T(8,128)(2,1)S(1)}, u32[]{:S(2)}, u32[]{:S(2)}) async-start(bf16[12,64,256]{2,1,0:T(8,128)(2,1)} %bitcast.10), calls=%async_computation.2 | async-start | bytes 786432 | tf_op jit(solution)/shard_map/all_to_all | solution.py:326
  129.5 1.9 %collective-permute-start.3 = (bf16[4,128,512]{2,1,0:T(8,128)(2,1)S(1)}, bf16[4,128,512]{2,1,0:T(8,128)(2,1)S(1)}, u32[]{:S(2)}, u32[]{:S(2)}) collective-permute-start(bf16[4,128,512]{2,1,0:T(8,128)(2,1)S(1)} %copy-done.14), channel_id=1, source_target_pairs={{0,1},{1,0},{2,3},{3,2},{4,5},{5,4},{6,7},{7,6},{8,9},{9,8},{10,11... | collective-permute-start | bytes 1572872 | tf_op jit(solution)/shard_map/ppermute | solution.py:314
  131.4 14.3 %all-to-all-done.2 = bf16[12,64,256]{2,1,0:T(8,128)(2,1)S(1)} async-done(((bf16[12,64,256]{2,1,0:T(8,128)(2,1)}), bf16[12,64,256]{2,1,0:T(8,128)(2,1)S(1)}, u32[]{:S(2)}, u32[]{:S(2)}) %all-to-all-start.2) | async-done | bytes 393248 | tf_op jit(solution)/shard_map/all_to_all | solution.py:326
  145.7 0.1 reduce_sum.12
  145.8 0.6 reshape.29
  146.4 11.3 %all-to-all-start.3 = ((bf16[32,2,256]{2,1,0:T(2,128)(2,1)}), bf16[32,2,256]{2,1,0:T(2,128)(2,1)S(1)}, u32[]{:S(2)}, u32[]{:S(2)}) async-start(bf16[32,2,256]{2,1,0:T(2,128)(2,1)} %reshape.29), calls=%async_computation.3 | async-start | bytes 65536 | tf_op jit(solution)/shard_map/all_to_all | solution.py:328
  157.8 0.0 collective-permute-done.3
  157.8 0.2 add_convert_fusion
  158.0 1.0 copy.14
  159.0 7.7 %all-to-all-done.3 = bf16[32,2,256]{2,1,0:T(2,128)(2,1)S(1)} async-done(((bf16[32,2,256]{2,1,0:T(2,128)(2,1)}), bf16[32,2,256]{2,1,0:T(2,128)(2,1)S(1)}, u32[]{:S(2)}, u32[]{:S(2)}) %all-to-all-start.3) | async-done | bytes 32800 | tf_op jit(solution)/shard_map/all_to_all | solution.py:328
  166.6 0.6 copy.15
  (17 shorter events, 0.1 us)
Async XLA Ops:
  0.6 86.4 %collective-permute-start.1 = (bf16[512,512]{1,0:T(8,128)(2,1)}, bf16[512,512]{1,0:T(8,128)(2,1)S(1)}, u32[]{:S(2)}, u32[]{:S(2)}) collective-permute-start(bf16[512,512]{1,0:T(8,128)(2,1)} %g_own.1), channel_id=1, source_target_pairs={{0,1},{1,0},{2,3},{3,2},{4,5},{5,4},{6,7},{7,6},{8,9},{9,8},{10,11... | collective-permute-start | bytes 1572872 | tf_op jit(solution)/shard_map/ppermute | solution.py:303
  2.6 0.7 copy-start.11
  2.6 0.7 copy-start.10
  2.7 0.7 copy-start.12
  3.3 1.0 copy-start
  4.4 1.0 copy-start.3
  5.4 0.9 copy-start.8
  6.4 0.9 copy-start.9
  7.3 5.1 %copy-start.4 = (bf16[512,512]{1,0:T(8,128)(2,1)S(1)}, bf16[512,512]{1,0:T(8,128)(2,1)}, u32[]{:S(2)}) copy-start(bf16[512,512]{1,0:T(8,128)(2,1)} %q_own.1) | copy-start | bytes 1572868
  9.9 77.1 %collective-permute-start.2 = (f32[8,512]{1,0:T(8,128)}, f32[8,512]{1,0:T(8,128)}, u32[]{:S(2)}, u32[]{:S(2)}) collective-permute-start(f32[8,512]{1,0:T(8,128)} %get-tuple-element.36.stat_own), channel_id=1, source_target_pairs={{0,1},{1,0},{2,3},{3,2},{4,5},{5,4},{6,7},{7,6},{8,9},{9,8},{10,11... | collective-permute-start | bytes 49160 | tf_op jit(solution)/shard_map/ppermute | solution.py:304
  12.4 74.6 %collective-permute-start = (bf16[512,512]{1,0:T(8,128)(2,1)S(1)}, bf16[512,512]{1,0:T(8,128)(2,1)}, u32[]{:S(2)}, u32[]{:S(2)}) collective-permute-start(bf16[512,512]{1,0:T(8,128)(2,1)S(1)} %copy-done.4), channel_id=1, source_target_pairs={{0,1},{1,0},{2,3},{3,2},{4,5},{5,4},{6,7},{7,6},{8,9},{9,8},{10,11... | collective-permute-start | bytes 1572872 | tf_op jit(solution)/shard_map/ppermute | solution.py:302
  68.4 19.4 %copy-start.1 = (bf16[512,512]{1,0:T(8,128)(2,1)S(1)}, bf16[512,512]{1,0:T(8,128)(2,1)}, u32[]{:S(2)}) copy-start(bf16[512,512]{1,0:T(8,128)(2,1)} %g_own.1) | copy-start | bytes 1572868
  87.0 0.8 copy-start.6
  87.8 1.0 copy-start.5
  88.8 1.0 copy-start.7
  104.7 1.0 copy-start.2
  105.7 0.8 copy-start.13
  106.5 17.2 %copy-start.15 = (bf16[4,20,16,256]{3,2,1,0:T(8,128)(2,1)S(1)}, bf16[4,20,16,256]{3,2,1,0:T(8,128)(2,1)}, u32[]{:S(2)}) copy-start(bf16[4,20,16,256]{3,2,1,0:T(8,128)(2,1)} %get-tuple-element.41) | copy-start | bytes 1966084
  106.5 17.2 %all-to-all-start.1 = ((bf16[4,28,16,256]{3,2,1,0:T(8,128)(2,1)}), bf16[4,28,16,256]{3,2,1,0:T(8,128)(2,1)S(1)}, u32[]{:S(2)}, u32[]{:S(2)}) async-start(bf16[4,28,16,256]{3,2,1,0:T(8,128)(2,1)} %copy-done.2), calls=%async_computation.1 | async-start | bytes 1835008 | tf_op jit(solution)/shard_map/all_to_all | solution.py:316
  112.0 0.6 copy-start.16
  125.7 3.7 %copy-start.14 = (bf16[4,128,512]{2,1,0:T(8,128)(2,1)S(1)}, bf16[4,128,512]{2,1,0:T(8,128)(2,1)}, u32[]{:S(2)}) copy-start(bf16[4,128,512]{2,1,0:T(8,128)(2,1)} %copy-done.13) | copy-start | bytes 1572868
  125.8 20.0 %all-to-all-start.2 = ((bf16[12,64,256]{2,1,0:T(8,128)(2,1)}), bf16[12,64,256]{2,1,0:T(8,128)(2,1)S(1)}, u32[]{:S(2)}, u32[]{:S(2)}) async-start(bf16[12,64,256]{2,1,0:T(8,128)(2,1)} %bitcast.10), calls=%async_computation.2 | async-start | bytes 786432 | tf_op jit(solution)/shard_map/all_to_all | solution.py:326
  129.5 28.3 %collective-permute-start.3 = (bf16[4,128,512]{2,1,0:T(8,128)(2,1)S(1)}, bf16[4,128,512]{2,1,0:T(8,128)(2,1)S(1)}, u32[]{:S(2)}, u32[]{:S(2)}) collective-permute-start(bf16[4,128,512]{2,1,0:T(8,128)(2,1)S(1)} %copy-done.14), channel_id=1, source_target_pairs={{0,1},{1,0},{2,3},{3,2},{4,5},{5,4},{6,7},{7,6},{8,9},{9,8},{10,11... | collective-permute-start | bytes 1572872 | tf_op jit(solution)/shard_map/ppermute | solution.py:314
  146.4 20.2 %all-to-all-start.3 = ((bf16[32,2,256]{2,1,0:T(2,128)(2,1)}), bf16[32,2,256]{2,1,0:T(2,128)(2,1)S(1)}, u32[]{:S(2)}, u32[]{:S(2)}) async-start(bf16[32,2,256]{2,1,0:T(2,128)(2,1)} %reshape.29), calls=%async_computation.3 | async-start | bytes 65536 | tf_op jit(solution)/shard_map/all_to_all | solution.py:328

commit v3 on v2

--- a/solution.py
+++ b/solution.py
@@ -19,6 +19,8 @@
 SLOTS = 28
 INFO_ROWS = 16
 PIECES = 2
+TERMS = 3
+TERM_ROWS = 32
 
 
 def dot_nt(a, b):
@@ -29,14 +31,29 @@
     return lax.dot_general(a, b, (((1,), (0,)), ((), ())), preferred_element_type=jnp.float32)
 
 
-def ready_kernel(doc_ids, block_docs, where, keys, values, outputs, grads, lse, both, stats, table, order, tally,
-                 *, owners, cores, cols, heads, head_size):
+def in_hbm(*arrays):
+    return [pltpu.with_memory_space_constraint(a, pltpu.HBM) for a in arrays]
+
+
+def ready_kernel(doc_ids, block_docs, where, keys, values, queries, outputs, grads, lse, both, stats, swap, table, order,
+                 tally, key_buf, value_buf, out_buf, grad_buf, terms, sems, *, owners, cores, cols, heads, head_size):
     blocks = block_docs.shape[0]
     block_rows = keys.shape[0]
     tok = grads.shape[0]
     half_rows = block_rows // cores
     piece = half_rows // (owners * cols)
     core, group = where[0], where[1]
+    lanes = pl.ds(pl.multiple_of(group * head_size, head_size), head_size)
+    copies = [
+        pltpu.make_async_copy(grads, grad_buf, sems.at[0]),
+        pltpu.make_async_copy(outputs, out_buf, sems.at[1]),
+        pltpu.make_async_copy(keys.at[:, lanes], key_buf, sems.at[2]),
+        pltpu.make_async_copy(values.at[:, lanes], value_buf, sems.at[3]),
+        pltpu.make_async_copy(queries, swap.at[:tok, :], sems.at[4]),
+        pltpu.make_async_copy(grads, swap.at[tok:2 * tok, :], sems.at[5]),
+    ]
+    for copy in copies:
+        copy.start()
 
     for d in range(DOC_SLOTS + 1):
         tally[d] = 0
@@ -64,56 +81,82 @@
     order[blocks] = first
     order[blocks + 1] = count
 
+    copies[0].wait()
+    copies[1].wait()
+    lane = lax.broadcasted_iota(jnp.int32, (tok, head_size), 1)
+    wide = jnp.zeros((tok, head_size), jnp.float32)
+    for h in range(heads):
+        span = slice(h * head_size, (h + 1) * head_size)
+        product = grad_buf[:, span].astype(jnp.float32) * out_buf[:, span].astype(jnp.float32)
+        wide = jnp.where(lane == h, jnp.sum(product, axis=1, keepdims=True), wide)
+    full = jnp.concatenate([wide.T[:heads, :], lse[...]], axis=0)
+    stats[...] = full
+    terms[...] = jnp.zeros_like(terms)
+    for t in range(TERMS):
+        term = full.astype(jnp.bfloat16)
+        terms[t * 2 * heads:(t + 1) * 2 * heads, :] = term
+        full = full - term.astype(jnp.float32)
+    last = pltpu.make_async_copy(terms, swap.at[2 * tok:, :], sems.at[6])
+    last.start()
+
     at = lax.broadcasted_iota(jnp.int32, (half_rows, block_rows), 0)
     row = lax.broadcasted_iota(jnp.int32, (half_rows, block_rows), 1)
     col, owner, sub = at // (owners * piece), at // piece % owners, at % piece
     pick = (row == ((owner * cores + core) * cols + col) * piece + sub).astype(jnp.float32).astype(jnp.bfloat16)
-    lanes = pl.ds(pl.multiple_of(group * head_size, head_size), head_size)
-    both[:half_rows, :head_size] = dot_nn(pick, keys[:, lanes]).astype(jnp.bfloat16)
-    both[:half_rows, head_size:] = dot_nn(pick, values[:, lanes]).astype(jnp.bfloat16)
+    copies[2].wait()
+    copies[3].wait()
+    both[:half_rows, :head_size] = dot_nn(pick, key_buf[...]).astype(jnp.bfloat16)
+    both[:half_rows, head_size:] = dot_nn(pick, value_buf[...]).astype(jnp.bfloat16)
     lane = lax.broadcasted_iota(jnp.int32, (INFO_ROWS, 2 * head_size), 1)
     info = jnp.where(lane == 0, first, jnp.where(lane == 1, count, 0))
     both[half_rows:, :] = info.astype(jnp.float32).astype(jnp.bfloat16)
-
-    lane = lax.broadcasted_iota(jnp.int32, (tok, head_size), 1)
-    wide = jnp.zeros((tok, head_size), jnp.float32)
-    for h in range(heads):
-        span = slice(h * head_size, (h + 1) * head_size)
-        product = grads[:, span].astype(jnp.float32) * outputs[:, span].astype(jnp.float32)
-        wide = jnp.where(lane == h, jnp.sum(product, axis=1, keepdims=True), wide)
-    stats[:heads, :] = wide.T[:heads, :]
-    stats[heads:, :] = lse[...]
-
-
-def ready(doc_ids, block_docs, where, keys, values, outputs, grads, lse, owners, cores, cols, interpret=False):
+    copies[4].wait()
+    copies[5].wait()
+    last.wait()
+
+
+def ready(doc_ids, block_docs, where, keys, values, queries, outputs, grads, lse, owners, cores, cols, interpret=False):
     heads, tok = lse.shape
-    head_size = grads.shape[1] // heads
+    width = grads.shape[1]
+    head_size = width // heads
     blocks = block_docs.shape[0]
-    half_rows = keys.shape[0] // cores
+    block_rows = keys.shape[0]
+    half_rows = block_rows // cores
     smem = pl.BlockSpec(memory_space=pltpu.SMEM)
     vmem = pl.BlockSpec(memory_space=pltpu.VMEM)
+    hbm = pl.BlockSpec(memory_space=pltpu.HBM)
     return pl.pallas_call(
         functools.partial(
             ready_kernel, owners=owners, cores=cores, cols=cols, heads=heads, head_size=head_size
         ),
-        in_specs=[smem] * 3 + [vmem] * 5,
-        out_specs=[vmem] * 2 + [smem] * 2,
+        in_specs=[smem] * 3 + [hbm] * 5 + [vmem],
+        out_specs=[vmem] * 2 + [hbm] + [smem] * 2,
         out_shape=[
             jax.ShapeDtypeStruct((half_rows + INFO_ROWS, 2 * head_size), jnp.bfloat16),
             jax.ShapeDtypeStruct((2 * heads, tok), jnp.float32),
+            pltpu.HBM((2 * tok + TERM_ROWS, width), jnp.bfloat16),
             jax.ShapeDtypeStruct((blocks,), jnp.int32),
             jax.ShapeDtypeStruct((blocks + 2,), jnp.int32),
         ],
-        scratch_shapes=[pltpu.SMEM((DOC_SLOTS + 1,), jnp.int32)],
+        scratch_shapes=[
+            pltpu.SMEM((DOC_SLOTS + 1,), jnp.int32),
+            pltpu.VMEM((block_rows, head_size), jnp.bfloat16),
+            pltpu.VMEM((block_rows, head_size), jnp.bfloat16),
+            pltpu.VMEM((tok, width), jnp.bfloat16),
+            pltpu.VMEM((tok, width), jnp.bfloat16),
+            pltpu.VMEM((TERM_ROWS, width), jnp.bfloat16),
+            pltpu.SemaphoreType.DMA((7,)),
+        ],
         compiler_params=pltpu.CompilerParams(vmem_limit_bytes=12 << 20),
         interpret=interpret,
-    )(doc_ids, block_docs, where, keys, values, outputs, grads, lse)
-
-
-def grad_kernel(doc_ids, block_docs, order, plane, q_own, q_oth, g_own, g_oth, stat_own, stat_oth, docs, *refs,
+    )(doc_ids, block_docs, where, *in_hbm(keys, values, queries, outputs, grads), lse)
+
+
+def grad_kernel(doc_ids, block_docs, order, plane, queries, grads, swapped, stat_own, docs, *refs,
                 heads, head_size, half_rows, pieces):
     gathered, refs = refs[:pieces], refs[pieces:]
-    dq_own, dq_oth, pack, rest, near, lse_doc, dq_acc, k_grp, v_grp, kt_grp, dk_acc, dv_acc = refs
+    dq_own, dq_out, pack_out, rest_out, near = refs[:5]
+    lse_doc, dq_acc, dq_oth, pack, rest, q_all, g_all, terms, stats, k_grp, v_grp, kt_grp, dk_acc, dv_acc, sems = refs[5:]
     blocks = block_docs.shape[0]
     tile = half_rows + INFO_ROWS
     cols, piece_rows, _ = gathered[0].shape
@@ -123,6 +166,17 @@
     scaling = head_size ** (-0.5)
     log2e = math.log2(math.e)
     first, count = order[blocks], order[blocks + 1]
+    loads = [pltpu.make_async_copy(swapped.at[2 * tok:, :], terms, sems.at[0])]
+    for h in range(heads):
+        span = slice(h * head_size, (h + 1) * head_size)
+        loads += [
+            pltpu.make_async_copy(queries.at[:, span], q_all.at[h], sems.at[1 + h]),
+            pltpu.make_async_copy(grads.at[:, span], g_all.at[h], sems.at[1 + heads + h]),
+            pltpu.make_async_copy(swapped.at[:tok, span], q_all.at[heads + h], sems.at[1 + 2 * heads + h]),
+            pltpu.make_async_copy(swapped.at[tok:2 * tok, span], g_all.at[heads + h], sems.at[1 + 3 * heads + h]),
+        ]
+    for load in loads:
+        load.start()
 
     lane = lax.broadcasted_iota(jnp.int32, (INFO_ROWS, head_size), 1)
     most = jnp.zeros((INFO_ROWS, head_size), jnp.float32)
@@ -137,14 +191,25 @@
         near[cols + col] = jnp.max(jnp.where(lane == 1, mate, 0.0)).astype(jnp.int32)
     near[2 * cols] = jnp.max(jnp.where(lane == 1, most, 0.0)).astype(jnp.int32)
 
+    loads[0].wait()
+    theirs = jnp.zeros((2 * heads, tok), jnp.float32)
+    for t in range(TERMS - 1, -1, -1):
+        theirs = theirs + terms[t * 2 * heads:(t + 1) * 2 * heads, :].astype(jnp.float32)
+    stats[:heads, :] = stat_own[:heads, :]
+    stats[heads:, :] = theirs[:heads]
+    lse_all = jnp.concatenate([stat_own[heads:, :], theirs[heads:]], axis=0) * log2e
     doc_row = docs[...]
     for d in range(DOC_SLOTS):
-        inside = doc_row == d
-        for s, stat in enumerate((stat_own, stat_oth)):
-            lse_doc[d, s * heads:(s + 1) * heads, :] = jnp.where(inside, stat[heads:, :] * log2e, MASKED)
+        lse_doc[d] = jnp.where(doc_row == d, lse_all, MASKED)
     dq_acc[...] = jnp.zeros_like(dq_acc)
     pack[...] = jnp.zeros_like(pack)
-    rest[...] = jnp.zeros_like(rest)
+
+    @pl.when(count > SLOTS)
+    def _():
+        rest[...] = jnp.zeros_like(rest)
+
+    for load in loads[1:]:
+        load.wait()
 
     def group_step(grp, carry):
         base = grp * GROUP
@@ -164,31 +229,39 @@
         kt_grp[...] = k_grp[...].T
         dk_acc[...] = jnp.zeros_like(dk_acc)
         dv_acc[...] = jnp.zeros_like(dv_acc)
-        for start in range(0, tok, CHUNK):
-            toks = slice(start, start + CHUNK)
-
-            @pl.when((group_docs[0] <= doc_ids[start + CHUNK - 1]) & (group_docs[-1] >= doc_ids[start]))
+        wanted = [
+            (group_docs[0] <= doc_ids[start + CHUNK - 1]) & (group_docs[-1] >= doc_ids[start])
+            for start in range(0, tok, CHUNK)
+        ]
+
+        def work(toks):
+            for h in range(2 * heads):
+                query = q_all[h, toks, :]
+                grad = g_all[h, toks, :]
+                delta = stats[h:h + 1, toks]
+                score = dot_nt(k_grp[...], query)
+                dprob = dot_nt(v_grp[...], grad)
+                prob_low, dscore = [], []
+                for s in range(GROUP):
+                    rows = slice(s * half_rows, (s + 1) * half_rows)
+                    shift = lse_doc[slot_docs[s], h:h + 1, toks]
+                    prob = jnp.exp2(score[rows] * (scaling * log2e) - shift)
+                    prob_low.append(prob.astype(jnp.bfloat16))
+                    dscore.append((prob * (dprob[rows] - delta) * scaling).astype(jnp.bfloat16))
+                low, ds = jnp.concatenate(prob_low, axis=0), jnp.concatenate(dscore, axis=0)
+                dk_acc[...] += dot_nn(ds, query)
+                dv_acc[...] += dot_nn(low, grad)
+                dq_acc[h, :, toks] += dot_nn(kt_grp[...], ds)
+
+        @pl.when(wanted[0] & wanted[1])
+        def _():
+            work(slice(0, tok))
+
+        for i, other in ((0, 1), (1, 0)):
+
+            @pl.when(wanted[i] & jnp.logical_not(wanted[other]))
             def _():
-                for h in range(2 * heads):
-                    q_ref, g_ref, stat = (q_own, g_own, stat_own) if h < heads else (q_oth, g_oth, stat_oth)
-                    at = (h % heads) * head_size
-                    query = q_ref[toks, at:at + head_size]
-                    grad = g_ref[toks, at:at + head_size]
-                    delta = stat[h % heads:h % heads + 1, toks]
-                    score = dot_nt(k_grp[...], query)
-                    dprob = dot_nt(v_grp[...], grad)
-                    probs, dscores = [], []
-                    for s in range(GROUP):
-                        rows = slice(s * half_rows, (s + 1) * half_rows)
-                        stats = lse_doc[slot_docs[s], h:h + 1, toks]
-                        prob = jnp.exp2(score[rows] * (scaling * log2e) - stats)
-                        probs.append(prob.astype(jnp.bfloat16))
-                        dscores.append((prob * (dprob[rows] - delta) * scaling).astype(jnp.bfloat16))
-                    prob_low = jnp.concatenate(probs, axis=0)
-                    dscore = jnp.concatenate(dscores, axis=0)
-                    dk_acc[...] += dot_nn(dscore, query)
-                    dv_acc[...] += dot_nn(prob_low, grad)
-                    dq_acc[h, :, toks] += dot_nn(kt_grp[...], dscore)
+                work(slice(i * CHUNK, (i + 1) * CHUNK))
 
         def put(out, slot):
             for s in range(GROUP):
@@ -211,41 +284,68 @@
     for h in range(heads):
         dq_own[h] = dq_acc[h]
         dq_oth[h] = dq_acc[heads + h].astype(jnp.bfloat16)
-
-
-def local_grads(doc_ids, block_docs, order, plane, q_own, q_oth, g_own, g_oth, stat_own, stat_oth, gathered, half_rows,
+    stores = [
+        pltpu.make_async_copy(pack, pack_out, sems.at[0]),
+        pltpu.make_async_copy(dq_oth, dq_out, sems.at[1]),
+    ]
+    for store in stores:
+        store.start()
+    late = pltpu.make_async_copy(rest, rest_out, sems.at[2])
+
+    @pl.when(count > SLOTS)
+    def _():
+        late.start()
+        late.wait()
+
+    for store in stores:
+        store.wait()
+
+
+def local_grads(doc_ids, block_docs, order, plane, queries, grads, swapped, stat_own, gathered, half_rows,
                 interpret=False):
-    tok, width = q_own.shape
+    tok, width = queries.shape
     cols = gathered[0].shape[0]
     head_size = gathered[0].shape[2] // 2
     blocks = block_docs.shape[0]
     heads = width // head_size
     smem = pl.BlockSpec(memory_space=pltpu.SMEM)
     vmem = pl.BlockSpec(memory_space=pltpu.VMEM)
+    hbm = pl.BlockSpec(memory_space=pltpu.HBM)
     rows = GROUP * half_rows
+    turned = (heads, head_size, tok)
+    pack = (cols, SLOTS, half_rows // cols, 2 * head_size)
+    rest = (cols, blocks - SLOTS, half_rows // cols, 2 * head_size)
     return pl.pallas_call(
         functools.partial(grad_kernel, heads=heads, head_size=head_size, half_rows=half_rows, pieces=len(gathered)),
-        in_specs=[smem] * 4 + [vmem] * (7 + len(gathered)),
-        out_specs=[vmem] * 4 + [smem],
+        in_specs=[smem] * 4 + [hbm] * 2 + [pl.BlockSpec(memory_space=pl.ANY)] + [vmem] * (2 + len(gathered)),
+        out_specs=[vmem] + [hbm] * 3 + [smem],
         out_shape=[
-            jax.ShapeDtypeStruct((heads, head_size, tok), jnp.float32),
-            jax.ShapeDtypeStruct((heads, head_size, tok), jnp.bfloat16),
-            jax.ShapeDtypeStruct((cols, SLOTS, half_rows // cols, 2 * head_size), jnp.bfloat16),
-            jax.ShapeDtypeStruct((cols, blocks - SLOTS, half_rows // cols, 2 * head_size), jnp.bfloat16),
+            jax.ShapeDtypeStruct(turned, jnp.float32),
+            pltpu.HBM(turned, jnp.bfloat16),
+            pltpu.HBM(pack, jnp.bfloat16),
+            pltpu.HBM(rest, jnp.bfloat16),
             jax.ShapeDtypeStruct((2 * cols + 1,), jnp.int32),
         ],
         scratch_shapes=[
             pltpu.VMEM((DOC_SLOTS, 2 * heads, tok), jnp.float32),
             pltpu.VMEM((2 * heads, head_size, tok), jnp.float32),
+            pltpu.VMEM(turned, jnp.bfloat16),
+            pltpu.VMEM(pack, jnp.bfloat16),
+            pltpu.VMEM(rest, jnp.bfloat16),
+            pltpu.VMEM((2 * heads, tok, head_size), jnp.bfloat16),
+            pltpu.VMEM((2 * heads, tok, head_size), jnp.bfloat16),
+            pltpu.VMEM((TERM_ROWS, tok), jnp.bfloat16),
+            pltpu.VMEM((2 * heads, tok), jnp.float32),
             pltpu.VMEM((rows, head_size), jnp.bfloat16),
             pltpu.VMEM((rows, head_size), jnp.bfloat16),
             pltpu.VMEM((head_size, rows), jnp.bfloat16),
             pltpu.VMEM((rows, head_size), jnp.float32),
             pltpu.VMEM((rows, head_size), jnp.float32),
+            pltpu.SemaphoreType.DMA((1 + 4 * heads,)),
         ],
-        compiler_params=pltpu.CompilerParams(vmem_limit_bytes=24 << 20),
+        compiler_params=pltpu.CompilerParams(vmem_limit_bytes=32 << 20),
         interpret=interpret,
-    )(doc_ids, block_docs, order, plane, q_own, q_oth, g_own, g_oth, stat_own, stat_oth, doc_ids[None, :], *gathered)
+    )(doc_ids, block_docs, order, plane, *in_hbm(queries, grads), swapped, stat_own, doc_ids[None, :], *gathered)
 
 
 def spread_kernel(table, near, *refs, blocks):
@@ -296,12 +396,10 @@
     swap = [(i, cores - 1 - i) for i in range(cores)]
 
     where = jnp.stack([lax.axis_index("c"), lax.axis_index(("x", "yh"))]).astype(jnp.int32)
-    both, stat_own, table, order = ready(
-        doc_ids, image_docs, where, keys, values, outputs, out_grad, lse.T, owners, cores, cols
+    both, stat_own, swap_out, table, order = ready(
+        doc_ids, image_docs, where, keys, values, queries, outputs, out_grad, lse.T, owners, cores, cols
     )
-    q_oth = lax.ppermute(queries, "c", swap)
-    g_oth = lax.ppermute(out_grad, "c", swap)
-    stat_oth = lax.ppermute(stat_own, "c", swap)
+    swapped = lax.ppermute(swap_out, "c", swap)
 
     column = lax.all_gather(both, "z", axis=0, tiled=True)
     cut = column.shape[0] // PIECES
@@ -309,7 +407,7 @@
 
     plane = lax.axis_index("z").astype(jnp.int32).reshape(1)
     dq_own, dq_oth, pack, rest, near = local_grads(
-        doc_ids, image_docs, order, plane, queries, q_oth, out_grad, g_oth, stat_own, stat_oth, gathered, half_rows
+        doc_ids, image_docs, order, plane, queries, out_grad, swapped, stat_own, gathered, half_rows
     )
     dq_back = lax.ppermute(dq_oth, "c", swap)
 

time: 168 us -> 189 us (1.12)
  the two profiles are of different devices: /device:TPU:8 before, /device:TPU:64 now
where the time goes in v3:
time: 189 us; the launch traced here: 188 us
  blocking collectives  70.9 us (38%)
  Pallas kernels  43.5 us (23%)
  waiting for transfers between devices  34.9 us (18%)
  starting transfers between devices  31.6 us (17%)
  local copies, waits for them, and re-layouts  4.94 us (3%)
    all_gather x2, blocking collectives, body(): lax.all_gather(column[p * cut:(p + 1) * cut], 'yl', axis=0)  38.8 us
    pallas_call x1, Pallas kernels, ready(): pl.pallas_call(functools.partial(ready_kernel, owners=owners, cores=cores...  34.1 us
    all_gather x1, blocking collectives, body(): column = lax.all_gather(both, 'z', axis=0, tiled=True)  32.1 us
    all_to_all x1, waiting for transfers between devices, body(): shared = lax.all_to_all(pack, 'yl', 0, 0, tiled=True)  13.3 us
    all_to_all x1, waiting for transfers between devices, body(): lax.all_to_all(sums.reshape(planes, half_rows, 2 * head_size), 'z', 0, 0,...  13 us
    all_to_all x1, starting transfers between devices, body(): lax.all_to_all(sums.reshape(planes, half_rows, 2 * head_size), 'z', 0, 0,...  11.7 us
    all_to_all x1, waiting for transfers between devices, body(): lax.all_to_all(home.reshape(cols * owners, piece, 2 * head_size), ('yl',...  8.62 us
    all_to_all x1, starting transfers between devices, body(): lax.all_to_all(home.reshape(cols * owners, piece, 2 * head_size), ('yl',...  8.08 us
  transfers between devices with their start and end apart: 5, of which 3 were waited for; matrix products, arithmetic and copies ran while one was open for 1% of the time, Pallas kernels for 0%

profile of v3, /device:TPU:64, one launch (start us, length us, event | category | flops | bytes accessed | tf_op | source)
XLA Modules:
  0.0 187.6 jit_solution(11930187419391095628)
XLA Ops:
  0.6 0.1 pad_add_fusion.where
  0.7 0.0 copy-start
  0.7 0.7 copy-done
  1.4 0.0 copy-start.2
  1.4 0.7 copy-done.2
  2.1 0.0 copy-start.3
  2.1 0.7 copy-done.3
  2.7 34.1 %shard_map.95 = (bf16[80,256]{1,0:T(8,128)(2,1)S(1)}, f32[8,512]{1,0:T(8,128)S(1)}, bf16[1056,512]{1,0:T(8,128)(2,1)}, s32[48]{0:T(128)S(1)}, s32[50]{0:T(128)S(1)}) custom-call(s32[512]{0:T(512)S(1)} %copy-done, s32[48]{0:T(128)S(1)} %copy-done.3, s32[2]{0:T(128)S(1)} %pad_add_fusion.where, bf16[128,1024]{1,0:T(8,128)(2,1)} %keys.1, ...), custom_call_target="tpu_custom_call" | custom-call | tf_op jit(solution)/shard_map/pallas_call | solution.py:128
  36.9 1.9 %collective-permute-start = (bf16[1056,512]{1,0:T(8,128)(2,1)}, bf16[1056,512]{1,0:T(8,128)(2,1)S(1)}, u32[]{:S(2)}, u32[]{:S(2)}) collective-permute-start(bf16[1056,512]{1,0:T(8,128)(2,1)} %get-tuple-element.37), channel_id=1, source_target_pairs={{0,1},{1,0},{2,3},{3,2},{4,5},{5,4},{6,7},{7,6},{8,9},{9,8},{10,11... | collective-permute-start | bytes 3244040 | tf_op jit(solution)/shard_map/ppermute | solution.py:402
  38.8 32.1 %all_gather.15 = bf16[960,256]{1,0:T(8,128)(2,1)S(1)} all-gather(bf16[80,256]{1,0:T(8,128)(2,1)S(1)} %get-tuple-element.39), channel_id=1, replica_groups=mesh['z'=12,'yl'=4,'x'=4,'yh'=2,'c'=2] {'z'}, dimensions={0}, use_global_device_ids=true | all-gather | bytes 532480 | tf_op jit(solution)/shard_map/all_gather | solution.py:404
  71.0 0.0 copy-start.1
  71.0 0.0 copy-start.4
  71.0 21.2 %all-gather.1 = bf16[1920,256]{1,0:T(8,128)(2,1)S(1)} all-gather(bf16[480,256]{1,0:T(8,128)(2,1)S(1)} %get-tuple-element.52), channel_id=3, replica_groups=mesh['z'=12,'yl'=4,'x'=4,'yh'=2,'c'=2] {'yl'}, dimensions={0}, use_global_device_ids=true | all-gather | bytes 1228800 | tf_op jit(solution)/shard_map/all_gather | solution.py:406
  92.2 17.6 %all-gather = bf16[1920,256]{1,0:T(8,128)(2,1)S(1)} all-gather(bf16[480,256]{1,0:T(8,128)(2,1)S(1)} %get-tuple-element.53), channel_id=2, replica_groups=mesh['z'=12,'yl'=4,'x'=4,'yh'=2,'c'=2] {'yl'}, dimensions={0}, use_global_device_ids=true | all-gather | bytes 1228800 | tf_op jit(solution)/shard_map/all_gather | solution.py:406
  109.8 0.0 collective-permute-done.swapped
  109.8 0.0 copy-done.1
  109.8 0.0 copy-done.4
  109.8 7.3 %shard_map.96 = (f32[4,128,512]{2,1,0:T(8,128)S(1)}, bf16[4,128,512]{2,1,0:T(8,128)(2,1)}, bf16[4,28,16,256]{3,2,1,0:T(8,128)(2,1)}, bf16[4,20,16,256]{3,2,1,0:T(8,128)(2,1)}, s32[9]{0:T(128)S(1)}) custom-call(s32[512]{0:T(512)S(1)} %copy-done.1, s32[48]{0:T(128)S(1)} %copy-done.4, s32[50]{0:T(128)S(1)} %get-tuple-element.36.order, s32[1]{0:T(128)} %bitcast.3.plane, ...), custom_call_target="tpu_custom_call" | custom-call | tf_op jit(solution)/shard_map/pallas_call | solution.py:318
  117.1 0.0 copy-start.5
  117.1 8.0 %all-to-all-start.1 = ((bf16[4,28,16,256]{3,2,1,0:T(8,128)(2,1)}), bf16[4,28,16,256]{3,2,1,0:T(8,128)(2,1)S(1)}, u32[]{:S(2)}, u32[]{:S(2)}) async-start(bf16[4,28,16,256]{3,2,1,0:T(8,128)(2,1)} %get-tuple-element.45), calls=%async_computation.1 | async-start | bytes 1835008 | tf_op jit(solution)/shard_map/all_to_all | solution.py:414
  125.1 0.6 slice.11
  126.3 13.3 %all-to-all-done.1 = bf16[4,28,16,256]{3,2,1,0:T(8,128)(2,1)S(1)} async-done(((bf16[4,28,16,256]{3,2,1,0:T(8,128)(2,1)}), bf16[4,28,16,256]{3,2,1,0:T(8,128)(2,1)S(1)}, u32[]{:S(2)}, u32[]{:S(2)}) %all-to-all-start.1) | async-done | bytes 917536 | tf_op jit(solution)/shard_map/all_to_all | solution.py:414
  139.6 0.0 copy-done.5
  139.6 0.0 copy-start.6
  139.6 2.1 %conditional.1 = (bf16[48,16,256]{2,1,0:T(8,128)(2,1)}) conditional(s32[]{:T(128)} %bitcast.9, (bf16[4,20,16,256]{3,2,1,0:T(8,128)(2,1)S(1)}, s32[48]{0:T(128)S(1)}, s32[9]{0:T(128)S(1)}, bf16[4,28,16,256]{3,2,1,0:T(8,128)(2,1)S(1)}) %tuple.23, (s32[48]{0:T(128)S(1)}, s32[9]{0:T(128)S(1)}, bf16[4,28,16,256]{3,2,1,0:T(8,128)(2,1)S(1)}) %tuple.15), branch_computations={%region_0.0_spmd, %region_1.0_spmd} | conditional | bytes 1310728 | solution.py:423
  139.6 2.1 %branch_1_fun.1 = bf16[48,16,256]{2,1,0:T(8,128)(2,1)} custom-call(s32[48]{0:T(128)S(1)} %get-tuple-element.21.table, s32[9]{0:T(128)S(1)} %get-tuple-element.22.near, bf16[4,28,16,256]{3,2,1,0:T(8,128)(2,1)S(1)} %get-tuple-element.23.refs_0_), custom_call_target="tpu_custom_call" | custom-call | tf_op jit(solution)/shard_map/cond/branch_1_fun/pallas_call | solution.py:375
  141.7 11.7 %all-to-all-start.2 = ((bf16[12,64,256]{2,1,0:T(8,128)(2,1)}), bf16[12,64,256]{2,1,0:T(8,128)(2,1)S(1)}, u32[]{:S(2)}, u32[]{:S(2)}) async-start(bf16[12,64,256]{2,1,0:T(8,128)(2,1)} %bitcast.10), calls=%async_computation.2 | async-start | bytes 786432 | tf_op jit(solution)/shard_map/all_to_all | solution.py:424
  153.4 0.0 copy-done.6
  153.4 1.9 %collective-permute-start.1 = (bf16[4,128,512]{2,1,0:T(8,128)(2,1)S(1)}, bf16[4,128,512]{2,1,0:T(8,128)(2,1)S(1)}, u32[]{:S(2)}, u32[]{:S(2)}) collective-permute-start(bf16[4,128,512]{2,1,0:T(8,128)(2,1)S(1)} %copy-done.6), channel_id=1, source_target_pairs={{0,1},{1,0},{2,3},{3,2},{4,5},{5,4},{6,7},{7,6},{8,9},{9,8},{10,11... | collective-permute-start | bytes 1572872 | tf_op jit(solution)/shard_map/ppermute | solution.py:412
  155.3 13.0 %all-to-all-done.2 = bf16[12,64,256]{2,1,0:T(8,128)(2,1)S(1)} async-done(((bf16[12,64,256]{2,1,0:T(8,128)(2,1)}), bf16[12,64,256]{2,1,0:T(8,128)(2,1)S(1)}, u32[]{:S(2)}, u32[]{:S(2)}) %all-to-all-start.2) | async-done | bytes 393248 | tf_op jit(solution)/shard_map/all_to_all | solution.py:424
  168.3 0.1 reduce_sum.12
  168.4 0.6 reshape.29
  169.0 8.1 %all-to-all-start.3 = ((bf16[32,2,256]{2,1,0:T(2,128)(2,1)}), bf16[32,2,256]{2,1,0:T(2,128)(2,1)S(1)}, u32[]{:S(2)}, u32[]{:S(2)}) async-start(bf16[32,2,256]{2,1,0:T(2,128)(2,1)} %reshape.29), calls=%async_computation.3 | async-start | bytes 65536 | tf_op jit(solution)/shard_map/all_to_all | solution.py:426
  177.1 0.0 collective-permute-done.1
  177.1 0.2 add_convert_fusion
  177.3 1.0 copy.14
  178.3 8.6 %all-to-all-done.3 = bf16[32,2,256]{2,1,0:T(2,128)(2,1)S(1)} async-done(((bf16[32,2,256]{2,1,0:T(2,128)(2,1)}), bf16[32,2,256]{2,1,0:T(2,128)(2,1)S(1)}, u32[]{:S(2)}, u32[]{:S(2)}) %all-to-all-start.3) | async-done | bytes 32800 | tf_op jit(solution)/shard_map/all_to_all | solution.py:426
  186.9 0.6 copy.15
  (3 shorter events, 0.0 us)
Async XLA Ops:
  0.7 0.7 copy-start
  1.4 0.7 copy-start.2
  2.1 0.7 copy-start.3
  36.9 72.9 %collective-permute-start = (bf16[1056,512]{1,0:T(8,128)(2,1)}, bf16[1056,512]{1,0:T(8,128)(2,1)S(1)}, u32[]{:S(2)}, u32[]{:S(2)}) collective-permute-start(bf16[1056,512]{1,0:T(8,128)(2,1)} %get-tuple-element.37), channel_id=1, source_target_pairs={{0,1},{1,0},{2,3},{3,2},{4,5},{5,4},{6,7},{7,6},{8,9},{9,8},{10,11... | collective-permute-start | bytes 3244040 | tf_op jit(solution)/shard_map/ppermute | solution.py:402
  71.0 38.8 %copy-start.1 = (s32[512]{0:T(512)S(1)}, s32[512]{0:T(512)}, u32[]{:S(2)}) copy-start(s32[512]{0:T(512)} %doc_ids.3) | copy-start | bytes 6148
  71.0 38.8 %copy-start.4 = (s32[48]{0:T(128)S(1)}, s32[48]{0:T(128)}, u32[]{:S(2)}) copy-start(s32[48]{0:T(128)} %block_docs.3) | copy-start | bytes 580
  117.1 22.5 %copy-start.5 = (bf16[4,20,16,256]{3,2,1,0:T(8,128)(2,1)S(1)}, bf16[4,20,16,256]{3,2,1,0:T(8,128)(2,1)}, u32[]{:S(2)}) copy-start(bf16[4,20,16,256]{3,2,1,0:T(8,128)(2,1)} %get-tuple-element.43) | copy-start | bytes 1966084
  117.1 22.5 %all-to-all-start.1 = ((bf16[4,28,16,256]{3,2,1,0:T(8,128)(2,1)}), bf16[4,28,16,256]{3,2,1,0:T(8,128)(2,1)S(1)}, u32[]{:S(2)}, u32[]{:S(2)}) async-start(bf16[4,28,16,256]{3,2,1,0:T(8,128)(2,1)} %get-tuple-element.45), calls=%async_computation.1 | async-start | bytes 1835008 | tf_op jit(solution)/shard_map/all_to_all | solution.py:414
  139.6 13.8 %copy-start.6 = (bf16[4,128,512]{2,1,0:T(8,128)(2,1)S(1)}, bf16[4,128,512]{2,1,0:T(8,128)(2,1)}, u32[]{:S(2)}) copy-start(bf16[4,128,512]{2,1,0:T(8,128)(2,1)} %get-tuple-element.41) | copy-start | bytes 1572868
  141.7 26.6 %all-to-all-start.2 = ((bf16[12,64,256]{2,1,0:T(8,128)(2,1)}), bf16[12,64,256]{2,1,0:T(8,128)(2,1)S(1)}, u32[]{:S(2)}, u32[]{:S(2)}) async-start(bf16[12,64,256]{2,1,0:T(8,128)(2,1)} %bitcast.10), calls=%async_computation.2 | async-start | bytes 786432 | tf_op jit(solution)/shard_map/all_to_all | solution.py:424
  153.4 23.7 %collective-permute-start.1 = (bf16[4,128,512]{2,1,0:T(8,128)(2,1)S(1)}, bf16[4,128,512]{2,1,0:T(8,128)(2,1)S(1)}, u32[]{:S(2)}, u32[]{:S(2)}) collective-permute-start(bf16[4,128,512]{2,1,0:T(8,128)(2,1)S(1)} %copy-done.6), channel_id=1, source_target_pairs={{0,1},{1,0},{2,3},{3,2},{4,5},{5,4},{6,7},{7,6},{8,9},{9,8},{10,11... | collective-permute-start | bytes 1572872 | tf_op jit(solution)/shard_map/ppermute | solution.py:412
  169.0 17.9 %all-to-all-start.3 = ((bf16[32,2,256]{2,1,0:T(2,128)(2,1)}), bf16[32,2,256]{2,1,0:T(2,128)(2,1)S(1)}, u32[]{:S(2)}, u32[]{:S(2)}) async-start(bf16[32,2,256]{2,1,0:T(2,128)(2,1)} %reshape.29), calls=%async_computation.3 | async-start | bytes 65536 | tf_op jit(solution)/shard_map/all_to_all | solution.py:426

commit v4 on v3

--- a/solution.py
+++ b/solution.py
@@ -36,7 +36,7 @@
 
 
 def ready_kernel(doc_ids, block_docs, where, keys, values, queries, outputs, grads, lse, both, stats, swap, table, order,
-                 tally, key_buf, value_buf, out_buf, grad_buf, terms, sems, *, owners, cores, cols, heads, head_size):
+                 tally, key_buf, value_buf, out_buf, sems, *, owners, cores, cols, heads, head_size):
     blocks = block_docs.shape[0]
     block_rows = keys.shape[0]
     tok = grads.shape[0]
@@ -45,12 +45,11 @@
     core, group = where[0], where[1]
     lanes = pl.ds(pl.multiple_of(group * head_size, head_size), head_size)
     copies = [
-        pltpu.make_async_copy(grads, grad_buf, sems.at[0]),
+        pltpu.make_async_copy(grads, swap.at[tok:2 * tok, :], sems.at[0]),
         pltpu.make_async_copy(outputs, out_buf, sems.at[1]),
         pltpu.make_async_copy(keys.at[:, lanes], key_buf, sems.at[2]),
         pltpu.make_async_copy(values.at[:, lanes], value_buf, sems.at[3]),
         pltpu.make_async_copy(queries, swap.at[:tok, :], sems.at[4]),
-        pltpu.make_async_copy(grads, swap.at[tok:2 * tok, :], sems.at[5]),
     ]
     for copy in copies:
         copy.start()
@@ -87,17 +86,15 @@
     wide = jnp.zeros((tok, head_size), jnp.float32)
     for h in range(heads):
         span = slice(h * head_size, (h + 1) * head_size)
-        product = grad_buf[:, span].astype(jnp.float32) * out_buf[:, span].astype(jnp.float32)
+        product = swap[tok:2 * tok, span].astype(jnp.float32) * out_buf[:, span].astype(jnp.float32)
         wide = jnp.where(lane == h, jnp.sum(product, axis=1, keepdims=True), wide)
     full = jnp.concatenate([wide.T[:heads, :], lse[...]], axis=0)
     stats[...] = full
-    terms[...] = jnp.zeros_like(terms)
+    swap[2 * tok:, :] = jnp.zeros((TERM_ROWS, tok), jnp.bfloat16)
     for t in range(TERMS):
         term = full.astype(jnp.bfloat16)
-        terms[t * 2 * heads:(t + 1) * 2 * heads, :] = term
+        swap[2 * tok + t * 2 * heads:2 * tok + (t + 1) * 2 * heads, :] = term
         full = full - term.astype(jnp.float32)
-    last = pltpu.make_async_copy(terms, swap.at[2 * tok:, :], sems.at[6])
-    last.start()
 
     at = lax.broadcasted_iota(jnp.int32, (half_rows, block_rows), 0)
     row = lax.broadcasted_iota(jnp.int32, (half_rows, block_rows), 1)
@@ -111,8 +108,6 @@
     info = jnp.where(lane == 0, first, jnp.where(lane == 1, count, 0))
     both[half_rows:, :] = info.astype(jnp.float32).astype(jnp.bfloat16)
     copies[4].wait()
-    copies[5].wait()
-    last.wait()
 
 
 def ready(doc_ids, block_docs, where, keys, values, queries, outputs, grads, lse, owners, cores, cols, interpret=False):
@@ -130,11 +125,11 @@
             ready_kernel, owners=owners, cores=cores, cols=cols, heads=heads, head_size=head_size
         ),
         in_specs=[smem] * 3 + [hbm] * 5 + [vmem],
-        out_specs=[vmem] * 2 + [hbm] + [smem] * 2,
+        out_specs=[vmem] * 3 + [smem] * 2,
         out_shape=[
             jax.ShapeDtypeStruct((half_rows + INFO_ROWS, 2 * head_size), jnp.bfloat16),
             jax.ShapeDtypeStruct((2 * heads, tok), jnp.float32),
-            pltpu.HBM((2 * tok + TERM_ROWS, width), jnp.bfloat16),
+            jax.ShapeDtypeStruct((2 * tok + TERM_ROWS, width), jnp.bfloat16),
             jax.ShapeDtypeStruct((blocks,), jnp.int32),
             jax.ShapeDtypeStruct((blocks + 2,), jnp.int32),
         ],
@@ -143,9 +138,7 @@
             pltpu.VMEM((block_rows, head_size), jnp.bfloat16),
             pltpu.VMEM((block_rows, head_size), jnp.bfloat16),
             pltpu.VMEM((tok, width), jnp.bfloat16),
-            pltpu.VMEM((tok, width), jnp.bfloat16),
-            pltpu.VMEM((TERM_ROWS, width), jnp.bfloat16),
-            pltpu.SemaphoreType.DMA((7,)),
+            pltpu.SemaphoreType.DMA((5,)),
         ],
         compiler_params=pltpu.CompilerParams(vmem_limit_bytes=12 << 20),
         interpret=interpret,

time: 189 us -> 159 us (0.84)
  Pallas kernels: 43.5 us -> 22.8 us
  starting transfers between devices: 31.6 us -> 23.7 us
    pallas_call x1, Pallas kernels: 34.1 us -> 2.97 us  [ready(): pl.pallas_call(functools.partial(ready_kernel, owners=owners, cores=cores...]
    pallas_call x1, Pallas kernels: 7.27 us -> 17.8 us  [local_grads(): pl.pallas_call(functools.partial(grad_kernel, heads=heads, head_size=head...]
    all_to_all x1, starting transfers between devices: 7.96 us -> 3.83 us  [body(): shared = lax.all_to_all(pack, 'yl', 0, 0, tiled=True)]
    all_to_all x1, starting transfers between devices: 11.7 us -> 8.86 us  [body(): lax.all_to_all(sums.reshape(planes, half_rows, 2 * head_size), 'z', 0, 0,...]
  transfers between devices with their start and end apart: 5 -> 5, of which waited for: 3 -> 3; matrix products, arithmetic and copies ran while one was open for 1% -> 2% of each run, Pallas kernels for 0% -> 0%
where the time goes in v4:
time: 159 us
  blocking collectives  70.9 us (45%)
  waiting for transfers between devices  34.9 us (22%)
  starting transfers between devices  23.7 us (15%)
  Pallas kernels  22.8 us (14%)
  local copies, waits for them, and re-layouts  4.94 us (3%)
    all_gather x2, blocking collectives, body(): lax.all_gather(column[p * cut:(p + 1) * cut], 'yl', axis=0)  38.8 us
    all_gather x1, blocking collectives, body(): column = lax.all_gather(both, 'z', axis=0, tiled=True)  32.1 us
    pallas_call x1, Pallas kernels, local_grads(): pl.pallas_call(functools.partial(grad_kernel, heads=heads, head_size=head...  17.8 us
    all_to_all x1, waiting for transfers between devices, body(): shared = lax.all_to_all(pack, 'yl', 0, 0, tiled=True)  13.3 us
    all_to_all x1, waiting for transfers between devices, body(): lax.all_to_all(sums.reshape(planes, half_rows, 2 * head_size), 'z', 0, 0,...  13 us
    all_to_all x1, starting transfers between devices, body(): lax.all_to_all(sums.reshape(planes, half_rows, 2 * head_size), 'z', 0, 0,...  8.86 us
    all_to_all x1, waiting for transfers between devices, body(): lax.all_to_all(home.reshape(cols * owners, piece, 2 * head_size), ('yl',...  8.62 us
    all_to_all x1, starting transfers between devices, body(): lax.all_to_all(home.reshape(cols * owners, piece, 2 * head_size), ('yl',...  7.2 us
  transfers between devices with their start and end apart: 5, of which 3 were waited for; matrix products, arithmetic and copies ran while one was open for 2% of the time, Pallas kernels for 0%

profile of v4, /device:TPU:64, one launch (start us, length us, event | category | flops | bytes accessed | tf_op | source)
XLA Modules:
  0.0 159.0 jit_solution(7539613865048465118)
XLA Ops:
  0.6 0.1 pad_add_fusion.where
  0.7 0.0 copy-start
  0.7 0.7 copy-done
  1.4 0.0 copy-start.2
  1.4 0.7 copy-done.2
  2.1 0.0 copy-start.3
  2.1 0.7 copy-done.3
  2.7 3.0 %shard_map.95 = (bf16[80,256]{1,0:T(8,128)(2,1)S(1)}, f32[8,512]{1,0:T(8,128)S(1)}, bf16[1056,512]{1,0:T(8,128)(2,1)S(1)}, s32[48]{0:T(128)S(1)}, s32[50]{0:T(128)S(1)}) custom-call(s32[512]{0:T(512)S(1)} %copy-done, s32[48]{0:T(128)S(1)} %copy-done.3, s32[2]{0:T(128)S(1)} %pad_add_fusion.where, bf16[128,1024]{1,0:T(8,128)(2,1)} %keys.1, ...), custom_call_target="tpu_custom_call" | custom-call | tf_op jit(solution)/shard_map/pallas_call | solution.py:123
  5.7 1.9 %collective-permute-start = (bf16[1056,512]{1,0:T(8,128)(2,1)S(1)}, bf16[1056,512]{1,0:T(8,128)(2,1)S(1)}, u32[]{:S(2)}, u32[]{:S(2)}) collective-permute-start(bf16[1056,512]{1,0:T(8,128)(2,1)S(1)} %get-tuple-element.37), channel_id=1, source_target_pairs={{0,1},{1,0},{2,3},{3,2},{4,5},{5,4},{6,7},{7,6},{8,9},{9,8},{10,11... | collective-permute-start | bytes 3244040 | tf_op jit(solution)/shard_map/ppermute | solution.py:395
  7.7 32.1 %all_gather.15 = bf16[960,256]{1,0:T(8,128)(2,1)S(1)} all-gather(bf16[80,256]{1,0:T(8,128)(2,1)S(1)} %get-tuple-element.39), channel_id=1, replica_groups=mesh['z'=12,'yl'=4,'x'=4,'yh'=2,'c'=2] {'z'}, dimensions={0}, use_global_device_ids=true | all-gather | bytes 532480 | tf_op jit(solution)/shard_map/all_gather | solution.py:397
  39.8 0.0 copy-start.1
  39.8 0.0 copy-start.4
  39.9 21.2 %all-gather.1 = bf16[1920,256]{1,0:T(8,128)(2,1)S(1)} all-gather(bf16[480,256]{1,0:T(8,128)(2,1)S(1)} %get-tuple-element.52), channel_id=3, replica_groups=mesh['z'=12,'yl'=4,'x'=4,'yh'=2,'c'=2] {'yl'}, dimensions={0}, use_global_device_ids=true | all-gather | bytes 1228800 | tf_op jit(solution)/shard_map/all_gather | solution.py:399
  61.0 17.6 %all-gather = bf16[1920,256]{1,0:T(8,128)(2,1)S(1)} all-gather(bf16[480,256]{1,0:T(8,128)(2,1)S(1)} %get-tuple-element.53), channel_id=2, replica_groups=mesh['z'=12,'yl'=4,'x'=4,'yh'=2,'c'=2] {'yl'}, dimensions={0}, use_global_device_ids=true | all-gather | bytes 1228800 | tf_op jit(solution)/shard_map/all_gather | solution.py:399
  78.7 0.0 collective-permute-done.swapped
  78.7 0.0 copy-done.1
  78.7 0.0 copy-done.4
  78.7 17.8 %shard_map.96 = (f32[4,128,512]{2,1,0:T(8,128)S(1)}, bf16[4,128,512]{2,1,0:T(8,128)(2,1)}, bf16[4,28,16,256]{3,2,1,0:T(8,128)(2,1)}, bf16[4,20,16,256]{3,2,1,0:T(8,128)(2,1)}, s32[9]{0:T(128)S(1)}) custom-call(s32[512]{0:T(512)S(1)} %copy-done.1, s32[48]{0:T(128)S(1)} %copy-done.4, s32[50]{0:T(128)S(1)} %get-tuple-element.36.order, s32[1]{0:T(128)} %bitcast.3.plane, ...), custom_call_target="tpu_custom_call" | custom-call | tf_op jit(solution)/shard_map/pallas_call | solution.py:311
  96.4 0.0 copy-start.5
  96.4 3.8 %all-to-all-start.1 = ((bf16[4,28,16,256]{3,2,1,0:T(8,128)(2,1)}), bf16[4,28,16,256]{3,2,1,0:T(8,128)(2,1)S(1)}, u32[]{:S(2)}, u32[]{:S(2)}) async-start(bf16[4,28,16,256]{3,2,1,0:T(8,128)(2,1)} %get-tuple-element.45), calls=%async_computation.1 | async-start | bytes 1835008 | tf_op jit(solution)/shard_map/all_to_all | solution.py:407
  100.3 0.6 slice.11
  101.5 13.3 %all-to-all-done.1 = bf16[4,28,16,256]{3,2,1,0:T(8,128)(2,1)S(1)} async-done(((bf16[4,28,16,256]{3,2,1,0:T(8,128)(2,1)}), bf16[4,28,16,256]{3,2,1,0:T(8,128)(2,1)S(1)}, u32[]{:S(2)}, u32[]{:S(2)}) %all-to-all-start.1) | async-done | bytes 917536 | tf_op jit(solution)/shard_map/all_to_all | solution.py:407
  114.8 0.0 copy-done.5
  114.8 0.0 copy-start.6
  114.8 2.1 %conditional.1 = (bf16[48,16,256]{2,1,0:T(8,128)(2,1)}) conditional(s32[]{:T(128)} %bitcast.9, (bf16[4,20,16,256]{3,2,1,0:T(8,128)(2,1)S(1)}, s32[48]{0:T(128)S(1)}, s32[9]{0:T(128)S(1)}, bf16[4,28,16,256]{3,2,1,0:T(8,128)(2,1)S(1)}) %tuple.23, (s32[48]{0:T(128)S(1)}, s32[9]{0:T(128)S(1)}, bf16[4,28,16,256]{3,2,1,0:T(8,128)(2,1)S(1)}) %tuple.15), branch_computations={%region_0.0_spmd, %region_1.0_spmd} | conditional | bytes 1310728 | solution.py:416
  114.8 2.1 %branch_1_fun.1 = bf16[48,16,256]{2,1,0:T(8,128)(2,1)} custom-call(s32[48]{0:T(128)S(1)} %get-tuple-element.21.table, s32[9]{0:T(128)S(1)} %get-tuple-element.22.near, bf16[4,28,16,256]{3,2,1,0:T(8,128)(2,1)S(1)} %get-tuple-element.23.refs_0_), custom_call_target="tpu_custom_call" | custom-call | tf_op jit(solution)/shard_map/cond/branch_1_fun/pallas_call | solution.py:368
  116.9 8.9 %all-to-all-start.2 = ((bf16[12,64,256]{2,1,0:T(8,128)(2,1)}), bf16[12,64,256]{2,1,0:T(8,128)(2,1)S(1)}, u32[]{:S(2)}, u32[]{:S(2)}) async-start(bf16[12,64,256]{2,1,0:T(8,128)(2,1)} %bitcast.10), calls=%async_computation.2 | async-start | bytes 786432 | tf_op jit(solution)/shard_map/all_to_all | solution.py:417
  125.7 0.0 copy-done.6
  125.7 1.9 %collective-permute-start.1 = (bf16[4,128,512]{2,1,0:T(8,128)(2,1)S(1)}, bf16[4,128,512]{2,1,0:T(8,128)(2,1)S(1)}, u32[]{:S(2)}, u32[]{:S(2)}) collective-permute-start(bf16[4,128,512]{2,1,0:T(8,128)(2,1)S(1)} %copy-done.6), channel_id=1, source_target_pairs={{0,1},{1,0},{2,3},{3,2},{4,5},{5,4},{6,7},{7,6},{8,9},{9,8},{10,11... | collective-permute-start | bytes 1572872 | tf_op jit(solution)/shard_map/ppermute | solution.py:405
  127.7 13.0 %all-to-all-done.2 = bf16[12,64,256]{2,1,0:T(8,128)(2,1)S(1)} async-done(((bf16[12,64,256]{2,1,0:T(8,128)(2,1)}), bf16[12,64,256]{2,1,0:T(8,128)(2,1)S(1)}, u32[]{:S(2)}, u32[]{:S(2)}) %all-to-all-start.2) | async-done | bytes 393248 | tf_op jit(solution)/shard_map/all_to_all | solution.py:417
  140.7 0.1 reduce_sum.12
  140.7 0.6 reshape.29
  141.4 7.2 %all-to-all-start.3 = ((bf16[32,2,256]{2,1,0:T(2,128)(2,1)}), bf16[32,2,256]{2,1,0:T(2,128)(2,1)S(1)}, u32[]{:S(2)}, u32[]{:S(2)}) async-start(bf16[32,2,256]{2,1,0:T(2,128)(2,1)} %reshape.29), calls=%async_computation.3 | async-start | bytes 65536 | tf_op jit(solution)/shard_map/all_to_all | solution.py:419
  148.6 0.0 collective-permute-done.1
  148.6 0.2 add_convert_fusion
  148.8 1.0 copy.14
  149.8 8.6 %all-to-all-done.3 = bf16[32,2,256]{2,1,0:T(2,128)(2,1)S(1)} async-done(((bf16[32,2,256]{2,1,0:T(2,128)(2,1)}), bf16[32,2,256]{2,1,0:T(2,128)(2,1)S(1)}, u32[]{:S(2)}, u32[]{:S(2)}) %all-to-all-start.3) | async-done | bytes 32800 | tf_op jit(solution)/shard_map/all_to_all | solution.py:419
  158.4 0.6 copy.15
  (3 shorter events, 0.0 us)
Async XLA Ops:
  0.7 0.7 copy-start
  1.4 0.7 copy-start.2
  2.1 0.7 copy-start.3
  5.7 72.9 %collective-permute-start = (bf16[1056,512]{1,0:T(8,128)(2,1)S(1)}, bf16[1056,512]{1,0:T(8,128)(2,1)S(1)}, u32[]{:S(2)}, u32[]{:S(2)}) collective-permute-start(bf16[1056,512]{1,0:T(8,128)(2,1)S(1)} %get-tuple-element.37), channel_id=1, source_target_pairs={{0,1},{1,0},{2,3},{3,2},{4,5},{5,4},{6,7},{7,6},{8,9},{9,8},{10,11... | collective-permute-start | bytes 3244040 | tf_op jit(solution)/shard_map/ppermute | solution.py:395
  39.8 38.8 %copy-start.1 = (s32[512]{0:T(512)S(1)}, s32[512]{0:T(512)}, u32[]{:S(2)}) copy-start(s32[512]{0:T(512)} %doc_ids.3) | copy-start | bytes 6148
  39.8 38.8 %copy-start.4 = (s32[48]{0:T(128)S(1)}, s32[48]{0:T(128)}, u32[]{:S(2)}) copy-start(s32[48]{0:T(128)} %block_docs.3) | copy-start | bytes 580
  96.4 18.3 %copy-start.5 = (bf16[4,20,16,256]{3,2,1,0:T(8,128)(2,1)S(1)}, bf16[4,20,16,256]{3,2,1,0:T(8,128)(2,1)}, u32[]{:S(2)}) copy-start(bf16[4,20,16,256]{3,2,1,0:T(8,128)(2,1)} %get-tuple-element.43) | copy-start | bytes 1966084
  96.4 18.3 %all-to-all-start.1 = ((bf16[4,28,16,256]{3,2,1,0:T(8,128)(2,1)}), bf16[4,28,16,256]{3,2,1,0:T(8,128)(2,1)S(1)}, u32[]{:S(2)}, u32[]{:S(2)}) async-start(bf16[4,28,16,256]{3,2,1,0:T(8,128)(2,1)} %get-tuple-element.45), calls=%async_computation.1 | async-start | bytes 1835008 | tf_op jit(solution)/shard_map/all_to_all | solution.py:407
  114.8 11.0 %copy-start.6 = (bf16[4,128,512]{2,1,0:T(8,128)(2,1)S(1)}, bf16[4,128,512]{2,1,0:T(8,128)(2,1)}, u32[]{:S(2)}) copy-start(bf16[4,128,512]{2,1,0:T(8,128)(2,1)} %get-tuple-element.41) | copy-start | bytes 1572868
  116.9 23.8 %all-to-all-start.2 = ((bf16[12,64,256]{2,1,0:T(8,128)(2,1)}), bf16[12,64,256]{2,1,0:T(8,128)(2,1)S(1)}, u32[]{:S(2)}, u32[]{:S(2)}) async-start(bf16[12,64,256]{2,1,0:T(8,128)(2,1)} %bitcast.10), calls=%async_computation.2 | async-start | bytes 786432 | tf_op jit(solution)/shard_map/all_to_all | solution.py:417
  125.7 22.8 %collective-permute-start.1 = (bf16[4,128,512]{2,1,0:T(8,128)(2,1)S(1)}, bf16[4,128,512]{2,1,0:T(8,128)(2,1)S(1)}, u32[]{:S(2)}, u32[]{:S(2)}) collective-permute-start(bf16[4,128,512]{2,1,0:T(8,128)(2,1)S(1)} %copy-done.6), channel_id=1, source_target_pairs={{0,1},{1,0},{2,3},{3,2},{4,5},{5,4},{6,7},{7,6},{8,9},{9,8},{10,11... | collective-permute-start | bytes 1572872 | tf_op jit(solution)/shard_map/ppermute | solution.py:405
  141.4 17.0 %all-to-all-start.3 = ((bf16[32,2,256]{2,1,0:T(2,128)(2,1)}), bf16[32,2,256]{2,1,0:T(2,128)(2,1)S(1)}, u32[]{:S(2)}, u32[]{:S(2)}) async-start(bf16[32,2,256]{2,1,0:T(2,128)(2,1)} %reshape.29), calls=%async_computation.3 | async-start | bytes 65536 | tf_op jit(solution)/shard_map/all_to_all | solution.py:419
